TPU v7x, 256 devices: a whole 4x4x8 slice. The times are simulated.
256 devices in a mesh: rep: 16 (over z_lo, x), tp: 16 (over y, z_hi, core).
Axes of the slice: x: 4, y: 4, z: 8 (z_hi: 2, z_lo: 4; z = z_hi * 4 + z_lo), core: 2. Of those that a mesh axis runs over, the one named last changes fastest.
Arguments:
- queries: bfloat16 [16, 512, 4096], P('rep', None, 'tp'), may hold values from -120 to 120
- keys: bfloat16 [16, 512, 4096], P('rep', None, 'tp'), may hold values from -6 to 6
- values: bfloat16 [16, 512, 4096], P('rep', None, 'tp'), may hold values from -6 to 6
- out_weight: bfloat16 [16, 4096, 7168], P('rep', 'tp'), may hold values from -0.09375 to 0.09375
- cotangent: bfloat16 [16, 512, 7168], P('rep', 'tp'), may hold values from -6 to 6
- local_params: bfloat16 [16, 2, 128, 7168], P('rep', None, 'tp'), may hold values from -6 to 6
- global_params: float32 [2, 128, 7168], P(None, 'tp'), may hold values from -6 to 6
- momentum: float32 [2, 128, 7168], P(None, 'tp'), may hold values from -3 to 3
- frag_index: int32 [1], replicated, may hold values from 0 to 1
Outputs:
- branch_out: bfloat16 [16, 512, 7168], P('rep', 'tp')
- weight_grad: bfloat16 [16, 4096, 7168], P('rep', 'tp')
- query_grad: bfloat16 [16, 512, 4096], P('rep', None, 'tp')
- key_grad: bfloat16 [16, 512, 4096], P('rep', None, 'tp')
- value_grad: bfloat16 [16, 512, 4096], P('rep', None, 'tp')
- new_global: float32 [128, 7168], P('tp')
- new_momentum: float32 [128, 7168], P('tp')
All inputs are finite; a program needn't handle non-finite values.
Results may differ from a plain program's by a relative error of at most 0.017.
Values may be sent and summed in bfloat16 or wider, within the bound.
No kernel may reach another device: no remote copies, remote signals or barrier semaphores. Data moves between devices by JAX's collectives and lax.ppermute only.
A program may use at most 128 MiB of HBM per device.

v0:
```python
import jax
import jax.numpy as jnp
from jax import lax
from jax.sharding import PartitionSpec as P

HD = 128
LEN = 512
SEQS = 1


outer_momentum = 0.9
outer_rate = 0.7


def nesterov(outer_old, moment_old, summed):
    average = summed / lax.axis_size("rep")
    pseudo_grad = outer_old - average
    new_momentum = outer_momentum * moment_old + pseudo_grad
    new_global = outer_old - outer_rate * (outer_momentum * new_momentum + pseudo_grad)
    return (new_global, new_momentum)


def outer_update(local_params, global_params, momentum, frag_index):
    chosen = frag_index[0]
    local_sel = lax.dynamic_index_in_dim(local_params[0], chosen, 0, keepdims=False).astype(
        jnp.float32
    )
    outer_old = lax.dynamic_index_in_dim(global_params, chosen, 0, keepdims=False)
    moment_old = lax.dynamic_index_in_dim(momentum, chosen, 0, keepdims=False)
    summed = lax.psum(local_sel.astype(jnp.bfloat16), "rep").astype(jnp.float32)
    return nesterov(outer_old, moment_old, summed)


def inner_step(queries, keys, values, out_weight, cotangent):
    scale = HD ** (-0.5)
    head_cols = queries.shape[2]
    heads_here = head_cols // HD
    tokens = queries.shape[1]
    weight_here = out_weight[0]
    query_heads = queries[0].reshape(SEQS, LEN, heads_here, HD)
    key_heads = keys[0].reshape(SEQS, LEN, heads_here, HD)
    value_heads = values[0].reshape(SEQS, LEN, heads_here, HD)
    scores = (
        jnp.einsum("slhd,smhd->shlm", query_heads, key_heads, preferred_element_type=jnp.float32)
        * scale
    )
    causal = jnp.arange(LEN)[:, None] >= jnp.arange(LEN)[None, :]
    scores = jnp.where(causal[None, None], scores, -1e30)
    top = jnp.max(scores, axis=-1, keepdims=True)
    weights = jnp.exp(scores - top)
    probs = weights / jnp.sum(weights, axis=-1, keepdims=True)
    probs_half = probs.astype(jnp.bfloat16)
    context = jnp.einsum(
        "shlm,smhd->slhd", probs_half, value_heads, preferred_element_type=jnp.float32
    )
    context = context.astype(jnp.bfloat16).reshape(tokens, head_cols)
    context_rows = context
    branch_out = lax.psum_scatter(
        jnp.dot(context_rows, weight_here, preferred_element_type=jnp.float32).astype(jnp.bfloat16),
        "tp",
        scatter_dimension=0,
        tiled=True,
    )
    block_rows = lax.all_gather(cotangent[0], "tp", axis=0, tiled=True)
    part_grad = lax.dot_general(
        block_rows, weight_here, (((1,), (1,)), ((), ())), preferred_element_type=jnp.float32
    )
    context_acc = part_grad
    context_rows = context
    weight_acc = lax.dot_general(
        context_rows, block_rows, (((0,), (0,)), ((), ())), preferred_element_type=jnp.float32
    )
    context_acc, weight_acc = (context_acc, weight_acc)
    weight_grad = weight_acc.astype(jnp.bfloat16)
    context_grad = context_acc.astype(jnp.bfloat16).reshape(SEQS, LEN, heads_here, HD)
    probs_grad = jnp.einsum(
        "slhd,smhd->shlm", context_grad, value_heads, preferred_element_type=jnp.float32
    )
    inner = jnp.sum(probs * probs_grad, axis=-1, keepdims=True)
    score_grad = (probs * (probs_grad - inner) * scale).astype(jnp.bfloat16)
    query_grad = jnp.einsum(
        "shlm,smhd->slhd", score_grad, key_heads, preferred_element_type=jnp.float32
    )
    key_grad = jnp.einsum(
        "shlm,slhd->smhd", score_grad, query_heads, preferred_element_type=jnp.float32
    )
    value_grad = jnp.einsum(
        "shlm,slhd->smhd", probs_half, context_grad, preferred_element_type=jnp.float32
    )
    shaped = [
        g.astype(jnp.bfloat16).reshape(1, tokens, head_cols)
        for g in (query_grad, key_grad, value_grad)
    ]
    return (branch_out[None], weight_grad[None], shaped[0], shaped[1], shaped[2])


def shards(
    queries, keys, values, out_weight, cotangent, local_params, global_params, momentum, frag_index
):
    results = inner_step(queries, keys, values, out_weight, cotangent)
    new_global, new_momentum = outer_update(local_params, global_params, momentum, frag_index)
    return (results[0], results[1], results[2], results[3], results[4], new_global, new_momentum)


def solution(mesh):
    placed = (
        P("rep", None, "tp"),
        P("rep", None, "tp"),
        P("rep", None, "tp"),
        P("rep", "tp", None),
        P("rep", "tp", None),
        P("rep", None, "tp", None),
        P(None, "tp", None),
        P(None, "tp", None),
        P(),
    )
    return jax.shard_map(
        shards,
        mesh=mesh,
        in_specs=placed,
        out_specs=(
            P("rep", "tp", None),
            P("rep", "tp", None),
            P("rep", None, "tp"),
            P("rep", None, "tp"),
            P("rep", None, "tp"),
            P("tp", None),
            P("tp", None),
        ),
        check_vma=False,
    )
```

profile of v0, /device:TPU:128, one launch (start us, length us, event | category | flops | bytes accessed | tf_op | source)
XLA Modules:
  0.0 294.4 jit_solution(1788196400667213289)
XLA Ops:
  8.0 0.0 copy-start
  8.0 0.0 all-reduce.2.cloned.1.call-start
  8.8 0.2 copy-done
  8.9 0.7 dynamic-slice_bitcast_fusion
  9.6 0.0 all-reduce.2.cloned.1.call-update
  9.6 0.0 all-gather.3.cloned.1.call-start
  9.7 0.5 all-gather.3.cloned.1.call-update
  10.2 0.0 reduce-scatter.2.cloned.1.call-start
  10.2 1.1 copy.35
  11.3 1.1 copy.36
  12.4 0.0 copy-start.1
  12.5 1.1 reshape.115
  13.6 0.1 iota_compare_fusion
  13.7 0.0 copy-start.2
  13.7 2.3 fusion.47
  16.0 0.0 copy-done.1
  16.0 0.0 copy-done.2
  16.0 1.3 convolution_convert_fusion.2
  17.3 7.2 %convolution_convert_fusion = bf16[512,7168]{1,0:T(8,128)(2,1)} fusion(bf16[512,256]{0,1:T(8,128)(2,1)S(1)} %bitcast.75, bf16[1,256,7168]{2,1,0:T(8,128)(2,1)} %param.12), kind=kOutput, calls=%fused_computation.2 | convolution fusion | flops 1882718208 | bytes 11272192 | tf_op jit(solution)/shard_map/dot_general | solution.py:59
  24.5 0.0 copy-start.3
  24.5 0.0 copy-start.4
  24.5 0.0 reduce-scatter.2.cloned.1.call-update
  24.5 235.7 %all-reduce.2.cloned.1.call-done = bf16[8,7168]{1,0:T(8,128)(2,1)} async-done(((bf16[8,7168]{1,0:T(8,128)(2,1)}), bf16[8,7168]{1,0:T(8,128)(2,1)}) %all-reduce.2.cloned.1.call-update) | async-done | bytes 114704 | tf_op jit(solution)/shard_map/psum | solution.py:30
  260.2 0.0 copy-done.3
  260.2 0.0 copy-done.4
  260.2 1.7 bitcast_subtract_fusion
  262.0 0.0 all-gather.3.cloned.1.call-done
  262.0 6.2 %fusion.24 = bf16[512,256]{0,1:T(8,128)(2,1)S(1)} fusion(bf16[1,256,7168]{2,1,0:T(8,128)(2,1)} %param.12, bf16[1,512,7168]{2,1,0:T(8,128)(2,1)} %all-gather.3.cloned.1.call-done), kind=kOutput, calls=%fused_computation.20 | convolution fusion | flops 1879179264 | bytes 11272192 | tf_op jit(solution)/shard_map/dot_general | solution.py:65
  268.2 0.4 fusion.37
  268.6 3.3 %fusion.18 = bf16[2,512,128]{1,2,0:T(8,128)(2,1)S(1)} fusion(bf16[512,2,128]{0,2,1:T(8,128)(2,1)} %bitcast.85, f32[2,512,512]{1,2,0:T(8,128)S(1)} %fusion.37, f32[2,512,512]{1,2,0:T(8,128)} %get-tuple-element.17, f32[2,512]{1,0:T(2,128)S(1)} %get-tuple-element.16), kind=kOutput, calls=%fused_computation.18 | convolution fusion | flops 138020352 | bytes 4722688 | tf_op jit(solution)/shard_map/shlm,smhd->slhd/dot_general | solution.py:81
  271.9 0.8 copy.27
  272.8 3.1 %fusion.21 = bf16[2,512,128]{1,2,0:T(8,128)(2,1)S(1)} fusion(bf16[512,2,128]{0,2,1:T(8,128)(2,1)S(1)} %bitcast.81, f32[2,512,512]{1,2,0:T(8,128)S(1)} %fusion.37, f32[2,512,512]{1,2,0:T(8,128)} %get-tuple-element.17, f32[2,512]{1,0:T(2,128)S(1)} %get-tuple-element.16), kind=kOutput, calls=%fused_computation.19 | convolution fusion | flops 138020352 | bytes 4722688 | tf_op jit(solution)/shard_map/shlm,slhd->smhd/dot_general | solution.py:84
  275.9 0.8 copy.28
  276.7 2.4 convolution_convert_fusion.3
  279.1 0.8 copy.29
  279.9 7.0 %fusion.2 = bf16[1,256,7168]{2,1,0:T(8,128)(2,1)} fusion(bf16[512,256]{0,1:T(8,128)(2,1)S(1)} %bitcast.76, bf16[1,512,7168]{2,1,0:T(8,128)(2,1)} %all-gather.3.cloned.1.call-done), kind=kOutput, calls=%fused_computation.4 | convolution fusion | flops 1880883200 | bytes 11272192 | tf_op jit(solution)/shard_map/dot_general | solution.py:70
  286.9 0.0 reduce-scatter.2.cloned.1.call-done
Async XLA Ops:
  8.0 0.9 copy-start
  8.0 252.2 %all-reduce.2.cloned.1.call-start = ((), (), s32[]{:S(2)}) async-start(), calls=%async_computation.2 | async-start | bytes 229376 | tf_op jit(solution)/shard_map/psum | solution.py:30
  9.6 252.3 %all-gather.3.cloned.1.call-start = ((), (), s32[]{:S(2)}) async-start(), calls=%async_computation.3 | async-start | bytes 7798784 | tf_op jit(solution)/shard_map/all_gather | solution.py:64
  10.2 276.7 %reduce-scatter.2.cloned.1.call-start = ((), (), s32[]{:S(2)}) async-start(), calls=%async_computation.1 | async-start | bytes 7798784 | tf_op jit(solution)/shard_map/reduce_scatter | solution.py:58
  12.4 3.5 %copy-start.1 = (bf16[1,512,256]{1,2,0:T(8,128)(2,1)}, bf16[1,512,256]{1,2,0:T(8,128)(2,1)S(1)}, u32[]{:S(2)}) copy-start(bf16[1,512,256]{1,2,0:T(8,128)(2,1)S(1)} %copy.36) | copy-start | bytes 786436
  13.7 2.3 copy-start.2
  24.5 235.8 %copy-start.3 = (f32[2,8,7168]{2,1,0:T(8,128)S(1)}, f32[2,8,7168]{2,1,0:T(8,128)}, u32[]{:S(2)}) copy-start(f32[2,8,7168]{2,1,0:T(8,128)} %param.15) | copy-start | bytes 1376260
  24.5 235.8 %copy-start.4 = (f32[2,8,7168]{2,1,0:T(8,128)S(1)}, f32[2,8,7168]{2,1,0:T(8,128)}, u32[]{:S(2)}) copy-start(f32[2,8,7168]{2,1,0:T(8,128)} %param.16) | copy-start | bytes 1376260
Sparse Core Ops, SparseCore 0:
  12.2 247.9 all-reduce.1
Sparse Core Ops, SparseCore 1:
  12.8 86.0 all-gather.2
  103.8 130.9 reduce-scatter.1
where the time goes:
time: 295 us; the launch traced here: 294 us
  waiting for transfers between devices  236 us (80%)
  matrix products  33.2 us (11%)
  between operations  16.3 us (6%)
  local copies, waits for them, and re-layouts  6.67 us (2%)
    psum x1, waiting for transfers between devices, outer_update(): summed = lax.psum(local_sel.astype(jnp.bfloat16), 'rep').astype(jnp.float32)  236 us
    dot_general x1, matrix products, inner_step(): jnp.dot(context_rows, weight_here, preferred_element_type=jnp.float32)  7.17 us
    dot_general x1, matrix products, inner_step(): lax.dot_general(context_rows, block_rows, (((0,), (0,)), ((), ())), prefe...  7 us
    dot_general x1, matrix products, inner_step(): lax.dot_general(block_rows, weight_here, (((1,), (1,)), ((), ())), prefer...  6.22 us
  transfers between devices with their start and end apart: 3, of which 1 were waited for; matrix products, arithmetic and copies ran while one was open for 14% of the time, Pallas kernels for 0%

commit v1 on v0

v1 whole, which is shorter than its diff:
```python
import functools

import jax
import jax.numpy as jnp
from jax import lax
from jax.experimental import pallas as pl
from jax.experimental.pallas import tpu as pltpu
from jax.sharding import PartitionSpec as P

HD = 128
ROWS = 128
N_Y = 4
F32 = jnp.float32
BF16 = jnp.bfloat16

outer_momentum = 0.9
outer_rate = 0.7
ANY = pl.ANY
SMEM = pltpu.SMEM


def tp_index(y, z, c):
    return (y % N_Y) * 4 + z * 2 + c


def tp_moves(move):
    return [
        (tp_index(y, z, c), tp_index(*move(y, z, c)))
        for y in range(N_Y)
        for z in range(2)
        for c in range(2)
    ]


AHEAD = tp_moves(lambda y, z, c: (y + 1 - 2 * c, z, c))
BACK = tp_moves(lambda y, z, c: (y - 1 + 2 * c, z, c))
ACROSS = tp_moves(lambda y, z, c: (y, 1 - z, c))
OTHER_CORE = tp_moves(lambda y, z, c: (y, z, 1 - c))
REP_STEPS = [[(r, r ^ bit) for r in range(16)] for bit in (1, 2, 4, 8)]


def send(value, moves, axis="tp"):
    return lax.ppermute(value, axis, moves)


def forward_kernel(core_ref, q_ref, k_ref, v_ref, ctx_ref, keep_ref, give_ref, probs_ref):
    scale = HD ** (-0.5)
    core = core_ref[0]
    tokens = q_ref.shape[0]
    for i in range(tokens // ROWS):
        n = ROWS * (i + 1)
        mine = pl.ds(i * ROWS, ROWS)
        scores = lax.dot_general(
            q_ref[mine, :], k_ref[pl.ds(0, n), :], (((1,), (1,)), ((), ())), preferred_element_type=F32
        )
        row = lax.broadcasted_iota(jnp.int32, (ROWS, n), 0) + i * ROWS
        col = lax.broadcasted_iota(jnp.int32, (ROWS, n), 1)
        scores = jnp.where(row >= col, scores * scale, -1e30)
        top = jnp.max(scores, axis=-1, keepdims=True)
        weights = jnp.exp(scores - top)
        probs = weights * (1.0 / jnp.sum(weights, axis=-1, keepdims=True))
        probs_ref[0, mine, pl.ds(0, n)] = probs
        ctx = jnp.dot(probs.astype(BF16), v_ref[pl.ds(0, n), :], preferred_element_type=F32)
        ctx = ctx.astype(BF16)
        ctx_ref[mine, :] = ctx
        even = jnp.concatenate([ctx[0:32], ctx[64:96]], axis=0)
        odd = jnp.concatenate([ctx[32:64], ctx[96:128]], axis=0)
        half = pl.ds(i * (ROWS // 2), ROWS // 2)
        keep_ref[half, :] = jnp.where(core == 0, even, odd)
        give_ref[half, :] = jnp.where(core == 0, odd, even)


def attention_forward(core, q, k, v):
    tokens, cols = q.shape
    heads = cols // HD
    head = pl.BlockSpec((tokens, HD), lambda h: (0, h))
    half = pl.BlockSpec((tokens // 2, HD), lambda h: (0, h))
    return pl.pallas_call(
        forward_kernel,
        grid=(heads,),
        in_specs=[pl.BlockSpec(memory_space=SMEM), head, head, head],
        out_specs=[head, half, half, pl.BlockSpec((1, tokens, tokens), lambda h: (h, 0, 0))],
        out_shape=[
            jax.ShapeDtypeStruct((tokens, cols), BF16),
            jax.ShapeDtypeStruct((tokens // 2, cols), BF16),
            jax.ShapeDtypeStruct((tokens // 2, cols), BF16),
            jax.ShapeDtypeStruct((heads, tokens, tokens), F32),
        ],
        compiler_params=pltpu.CompilerParams(vmem_limit_bytes=32 << 20),
        cost_estimate=pl.CostEstimate(
            flops=4 * heads * tokens * tokens * HD, bytes_accessed=4 << 20, transcendentals=heads * tokens * tokens
        ),
        name="attention_forward",
    )(core, q, k, v)


def project_kernel(at_ref, mine_ref, theirs_ref, w_ref, w2_ref, *rest):
    outs, held = rest[:-1], rest[-1]
    part = jnp.dot(mine_ref[...], w_ref[...], preferred_element_type=F32)
    part += jnp.dot(theirs_ref[...], w2_ref[...], preferred_element_type=F32)
    held[...] = part.astype(BF16)
    for i, out in enumerate(outs):
        out[...] = held[pl.ds(pl.multiple_of(at_ref[i], 32), 32), :]


def project(at, mine, theirs, w, w2, blk=1024):
    rows, cols = mine.shape
    width = w.shape[1]
    whole = pl.BlockSpec((rows, cols), lambda j: (0, 0))
    weight = pl.BlockSpec((cols, blk), lambda j: (0, j))
    chunk = pl.BlockSpec((32, blk), lambda j: (0, j))
    n = rows // 32
    return pl.pallas_call(
        project_kernel,
        grid=(width // blk,),
        in_specs=[pl.BlockSpec(memory_space=SMEM), whole, whole, weight, weight],
        out_specs=[chunk] * n,
        out_shape=[jax.ShapeDtypeStruct((32, width), BF16)] * n,
        scratch_shapes=[pltpu.VMEM((rows, blk), BF16)],
        compiler_params=pltpu.CompilerParams(vmem_limit_bytes=32 << 20),
        cost_estimate=pl.CostEstimate(
            flops=4 * rows * cols * width, bytes_accessed=11 << 20, transcendentals=0
        ),
        name="project",
    )(at, mine, theirs, w, w2)


def weight_kernel(n, at_ref, ctx_ref, w_ref, *rest):
    pieces, (wg_ref, cg_ref, held, acc) = rest[:n], rest[n:]
    for i, piece in enumerate(pieces):
        held[pl.ds(pl.multiple_of(at_ref[i], 32), 32), :] = piece[...]
    block = held[...]
    wg = lax.dot_general(ctx_ref[...], block, (((0,), (0,)), ((), ())), preferred_element_type=F32)
    wg_ref[...] = wg.astype(BF16)
    part = lax.dot_general(block, w_ref[...], (((1,), (1,)), ((), ())), preferred_element_type=F32)
    j = pl.program_id(0)

    @pl.when(j == 0)
    def _():
        acc[...] = part

    @pl.when(j > 0)
    def _():
        acc[...] += part

    @pl.when(j == pl.num_programs(0) - 1)
    def _():
        cg_ref[...] = acc[...].astype(BF16)


def weight_and_context_grads(at, ctx, w, pieces, blk=1024):
    tokens, cols = ctx.shape
    width = w.shape[1]
    n = len(pieces)
    whole = pl.BlockSpec((tokens, cols), lambda j: (0, 0))
    weight = pl.BlockSpec((cols, blk), lambda j: (0, j))
    chunk = pl.BlockSpec((32, blk), lambda j: (0, j))
    return pl.pallas_call(
        functools.partial(weight_kernel, n),
        grid=(width // blk,),
        in_specs=[pl.BlockSpec(memory_space=SMEM), whole, weight] + [chunk] * n,
        out_specs=[weight, whole],
        out_shape=[jax.ShapeDtypeStruct((cols, width), BF16), jax.ShapeDtypeStruct((tokens, cols), BF16)],
        scratch_shapes=[pltpu.VMEM((tokens, blk), BF16), pltpu.VMEM((tokens, cols), F32)],
        compiler_params=pltpu.CompilerParams(vmem_limit_bytes=32 << 20),
        cost_estimate=pl.CostEstimate(
            flops=4 * tokens * cols * width, bytes_accessed=15 << 20, transcendentals=0
        ),
        name="weight_and_context_grads",
    )(at, ctx, w, *pieces)


def backward_kernel(q_ref, k_ref, v_ref, cg_ref, probs_ref, dq_ref, dk_ref, dv_ref, dk_acc, dv_acc):
    scale = HD ** (-0.5)
    tokens = q_ref.shape[0]
    blocks = tokens // ROWS
    for i in reversed(range(blocks)):
        n = ROWS * (i + 1)
        mine, seen = pl.ds(i * ROWS, ROWS), pl.ds(0, n)
        probs = probs_ref[0, mine, seen]
        cg = cg_ref[mine, :]
        probs_grad = lax.dot_general(
            cg, v_ref[seen, :], (((1,), (1,)), ((), ())), preferred_element_type=F32
        )
        inner = jnp.sum(probs * probs_grad, axis=-1, keepdims=True)
        score_grad = (probs * (probs_grad - inner) * scale).astype(BF16)
        dq_ref[mine, :] = jnp.dot(score_grad, k_ref[seen, :], preferred_element_type=F32).astype(BF16)
        dk = lax.dot_general(score_grad, q_ref[mine, :], (((0,), (0,)), ((), ())), preferred_element_type=F32)
        dv = lax.dot_general(probs.astype(BF16), cg, (((0,), (0,)), ((), ())), preferred_element_type=F32)
        if i == blocks - 1:
            dk_acc[...] = dk
            dv_acc[...] = dv
        else:
            dk_acc[seen, :] += dk
            dv_acc[seen, :] += dv
    dk_ref[...] = dk_acc[...].astype(BF16)
    dv_ref[...] = dv_acc[...].astype(BF16)


def attention_backward(q, k, v, cg, probs):
    tokens, cols = q.shape
    heads = cols // HD
    head = pl.BlockSpec((tokens, HD), lambda h: (0, h))
    return pl.pallas_call(
        backward_kernel,
        grid=(heads,),
        in_specs=[head] * 4 + [pl.BlockSpec((1, tokens, tokens), lambda h: (h, 0, 0))],
        out_specs=[head] * 3,
        out_shape=[jax.ShapeDtypeStruct((tokens, cols), BF16)] * 3,
        scratch_shapes=[pltpu.VMEM((tokens, HD), F32)] * 2,
        compiler_params=pltpu.CompilerParams(vmem_limit_bytes=32 << 20),
        cost_estimate=pl.CostEstimate(
            flops=8 * heads * tokens * tokens * HD, bytes_accessed=4 << 20, transcendentals=0
        ),
        name="attention_backward",
    )(q, k, v, cg, probs)


def add(*terms):
    total = terms[0].astype(F32)
    for term in terms[1:]:
        total = total + term.astype(F32)
    return total.astype(BF16)


def nesterov(outer_old, moment_old, summed):
    average = summed / lax.axis_size("rep")
    pseudo_grad = outer_old - average
    new_momentum = outer_momentum * moment_old + pseudo_grad
    new_global = outer_old - outer_rate * (outer_momentum * new_momentum + pseudo_grad)
    return (new_global, new_momentum)


def outer_update(local_params, global_params, momentum, frag_index):
    chosen = frag_index[0]
    part = lax.dynamic_index_in_dim(local_params[0], chosen, 0, keepdims=False)
    outer_old = lax.dynamic_index_in_dim(global_params, chosen, 0, keepdims=False)
    moment_old = lax.dynamic_index_in_dim(momentum, chosen, 0, keepdims=False)
    for moves in REP_STEPS[:-1]:
        part = lax.reduce_precision(part.astype(F32) + send(part, moves, "rep").astype(F32), 8, 7).astype(BF16)
        part = lax.optimization_barrier(part)
    summed = part.astype(F32) + send(part, REP_STEPS[-1], "rep").astype(F32)
    return nesterov(outer_old, moment_old, summed)


def shards(
    queries, keys, values, out_weight, cotangent, local_params, global_params, momentum, frag_index
):
    q, k, v, w, x = queries[0], keys[0], values[0], out_weight[0], cotangent[0]
    me = lax.axis_index("tp")
    y, z, c = me // 4, (me // 2) % 2, me % 2
    ahead = 1 - 2 * c

    far = send(x, ACROSS)
    near = [x]
    near.append(send(x, AHEAD))
    near.append(send(x, BACK))
    near.append(send(near[1], AHEAD))
    w2 = send(w, OTHER_CORE)

    core = jnp.reshape(c, (1,)).astype(jnp.int32)
    ctx, keep, give, probs = attention_forward(core, q, k, v)
    theirs = send(give, OTHER_CORE)
    at = [
        ((jnp.mod(y + hop * ahead, N_Y)) * 2 + zz) * 32 for zz in (z, 1 - z) for hop in (0, 1, 2, 3)
    ]
    parts = project(jnp.stack(at).astype(jnp.int32), keep, theirs, w, w2)
    own, other = parts[:4], parts[4:]

    def over_y(p):
        first = send(p[2], AHEAD)
        side = send(p[3], BACK)
        second = send(add(p[1], first), AHEAD)
        return second, side

    second, side = over_y(other)
    crossed = send(add(other[0], second, side), ACROSS)

    farther = [far]
    farther.append(send(far, AHEAD))
    farther.append(send(far, BACK))
    farther.append(send(farther[1], AHEAD))

    second, side = over_y(own)
    branch_out = add(own[0], second, side, crossed)

    mine = near + farther
    pieces = mine + [send(piece, OTHER_CORE) for piece in mine]
    token_at = [
        (jnp.mod(y + hop * sign, N_Y) * 4 + zz * 2 + cc) * 32
        for cc, sign in ((c, ahead), (1 - c, -ahead))
        for zz in (z, 1 - z)
        for hop in (0, -1, 1, -2)
    ]
    weight_grad, cg = weight_and_context_grads(jnp.stack(token_at).astype(jnp.int32), ctx, w, pieces)
    dq, dk, dv = attention_backward(q, k, v, cg, probs)
    new_global, new_momentum = outer_update(local_params, global_params, momentum, frag_index)
    return (branch_out[None], weight_grad[None], dq[None], dk[None], dv[None], new_global, new_momentum)


def solution(mesh):
    placed = (
        P("rep", None, "tp"),
        P("rep", None, "tp"),
        P("rep", None, "tp"),
        P("rep", "tp", None),
        P("rep", "tp", None),
        P("rep", None, "tp", None),
        P(None, "tp", None),
        P(None, "tp", None),
        P(),
    )
    return jax.shard_map(
        shards,
        mesh=mesh,
        in_specs=placed,
        out_specs=(
            P("rep", "tp", None),
            P("rep", "tp", None),
            P("rep", None, "tp"),
            P("rep", None, "tp"),
            P("rep", None, "tp"),
            P("tp", None),
            P("tp", None),
        ),
        check_vma=False,
    )
```

time: 295 us -> 117 us (0.40)
  the two profiles are of different devices: /device:TPU:128 before, /device:TPU:1 now
where the time goes in v1:
time: 117 us; the launch traced here: 116 us
  starting transfers between devices  54.5 us (47%)
  waiting for transfers between devices  28.8 us (25%)
  Pallas kernels  22.4 us (19%)
  local copies, waits for them, and re-layouts  6.01 us (5%)
  other arithmetic  3.22 us (3%)
  between operations  1.5 us (1%)
    ppermute x28, starting transfers between devices, send(): return lax.ppermute(value, axis, moves)  54.5 us
    ppermute x28, waiting for transfers between devices, send(): return lax.ppermute(value, axis, moves)  28.8 us
    pallas_call x1, Pallas kernels, weight_and_context_grads(): pl.pallas_call(functools.partial(weight_kernel, n), grid=(width // blk,),...  8.73 us
    pallas_call x1, Pallas kernels, project(): pl.pallas_call(project_kernel, grid=(width // blk,), in_specs=[pl.BlockSp...  6.58 us
    unnamed x22, local copies, waits for them, and re-layouts  4.93 us
    pallas_call x1, Pallas kernels, attention_backward(): pl.pallas_call(backward_kernel, grid=(heads,), in_specs=[head] * 4 + [pl....  3.86 us
    pallas_call x1, Pallas kernels, attention_forward(): pl.pallas_call(forward_kernel, grid=(heads,), in_specs=[pl.BlockSpec(memo...  3.21 us
  transfers between devices with their start and end apart: 28, of which 8 were waited for; matrix products, arithmetic and copies ran while one was open for 3% of the time, Pallas kernels for 19%

profile of v1, /device:TPU:1, one launch (start us, length us, event | category | flops | bytes accessed | tf_op | source)
XLA Modules:
  0.0 116.4 jit_solution(16985934167460005514)
XLA Ops:
  0.6 3.3 %collective-permute-start.1 = (bf16[256,7168]{1,0:T(8,128)(2,1)}, bf16[256,7168]{1,0:T(8,128)(2,1)}, u32[]{:S(2)}, u32[]{:S(2)}) collective-permute-start(bf16[256,7168]{1,0:T(8,128)(2,1)} %bitcast.55), channel_id=1, source_target_pairs={{0,1},{1,0},{2,3},{3,2},{4,5},{5,4},{6,7},{7,6},{8,9},{9,8},{10,11... | collective-permute-start | bytes 11010056 | tf_op jit(solution)/shard_map/ppermute | solution.py:43
  4.6 0.9 dynamic-slice_bitcast_fusion
  5.5 4.8 %collective-permute-done.24 = bf16[8,7168]{1,0:T(8,128)(2,1)S(1)} collective-permute-done((bf16[8,7168]{1,0:T(8,128)(2,1)S(1)}, bf16[8,7168]{1,0:T(8,128)(2,1)S(1)}, u32[]{:S(2)}, u32[]{:S(2)}) %collective-permute-start.24) | collective-permute-done | bytes 114720 | tf_op jit(solution)/shard_map/ppermute | solution.py:43
  10.3 0.9 reduce-precision_convert_fusion.2
  11.2 1.1 collective-permute-start.25
  12.3 6.9 %collective-permute-start.12 = (bf16[32,7168]{1,0:T(8,128)(2,1)}, bf16[32,7168]{1,0:T(8,128)(2,1)S(1)}, u32[]{:S(2)}, u32[]{:S(2)}) collective-permute-start(bf16[32,7168]{1,0:T(8,128)(2,1)} %bitcast.64), channel_id=1, source_target_pairs={{0,2},{1,3},{2,0},{3,1},{4,6},{5,7},{6,4},{7,5},{8,10},{9,11},{10,... | collective-permute-start | bytes 1376264 | tf_op jit(solution)/shard_map/ppermute | solution.py:43
  19.2 2.7 %collective-permute-start.9 = (bf16[32,7168]{1,0:T(8,128)(2,1)}, bf16[32,7168]{1,0:T(8,128)(2,1)S(1)}, u32[]{:S(2)}, u32[]{:S(2)}) collective-permute-start(bf16[32,7168]{1,0:T(8,128)(2,1)} %bitcast.65), channel_id=1, source_target_pairs={{0,4},{1,13},{2,6},{3,15},{4,8},{5,1},{6,10},{7,3},{8,12},{9,5},{1... | collective-permute-start | bytes 1376264 | tf_op jit(solution)/shard_map/ppermute | solution.py:43
  22.0 0.1 stack.86.at_ref
  22.1 0.1 stack.103.at_ref
  22.2 0.9 copy-done.2
  23.1 0.9 copy-done.4
  24.1 0.9 copy-done.6
  25.0 3.2 %attention_forward.1 = (bf16[512,256]{1,0:T(8,128)(2,1)S(1)}, bf16[256,256]{1,0:T(8,128)(2,1)S(1)}, bf16[256,256]{1,0:T(8,128)(2,1)S(1)}, f32[2,512,512]{2,1,0:T(8,128)S(1)}) custom-call(s32[1]{0:T(128)} %bitcast.8.core_ref, bf16[512,256]{1,0:T(8,128)(2,1)S(1)} %bitcast.58, bf16[512,256]{1,0:T(8,128)(2,1)S(1)} %bitcast.60, bf16[512,256]{1,0:T(8,128)(2,1)S(1)} %bitcast.62), custom_call_target="tpu_custom_call" | custom-call | flops 268435456 | bytes 4194304 | tf_op jit(solution)/shard_map/attention_forward/pallas_call | solution.py:78
  28.2 1.9 %collective-permute-start = (bf16[256,256]{1,0:T(8,128)(2,1)S(1)}, bf16[256,256]{1,0:T(8,128)(2,1)S(1)}, u32[]{:S(2)}, u32[]{:S(2)}) collective-permute-start(bf16[256,256]{1,0:T(8,128)(2,1)S(1)} %get-tuple-element.25), channel_id=1, source_target_pairs={{0,1},{1,0},{2,3},{3,2},{4,5},{5,4},{6,7},{7,6},{8,9},{9,8},{10,11... | collective-permute-start | bytes 393224 | tf_op jit(solution)/shard_map/ppermute | solution.py:43
  30.2 1.0 collective-permute-done.theirs_ref
  31.2 0.4 collective-permute-start.16
  31.5 0.7 collective-permute-start.26
  32.3 2.0 %copy-done = bf16[1,256,7168]{2,1,0:T(8,128)(2,1)S(1)} copy-done((bf16[1,256,7168]{2,1,0:T(8,128)(2,1)S(1)}, bf16[1,256,7168]{2,1,0:T(8,128)(2,1)}, u32[]{:S(2)}) %copy-start) | copy-done | bytes 3670040
  34.3 6.6 %project.1 = (bf16[32,7168]{1,0:T(8,128)(2,1)S(1)}, bf16[32,7168]{1,0:T(8,128)(2,1)S(1)}, bf16[32,7168]{1,0:T(8,128)(2,1)S(1)}, bf16[32,7168]{1,0:T(8,128)(2,1)S...) custom-call(s32[8]{0:T(128)S(1)} %stack.86.at_ref, ...), custom_call_target="tpu_custom_call" | custom-call | flops 1879048192 | bytes 11534336 | tf_op jit(solution)/shard_map/project/pallas_call | solution.py:113
  40.9 0.8 collective-permute-done.26
  41.7 2.7 %collective-permute-start.5 = (bf16[32,7168]{1,0:T(8,128)(2,1)S(1)}, bf16[32,7168]{1,0:T(8,128)(2,1)S(1)}, u32[]{:S(2)}, u32[]{:S(2)}) collective-permute-start(bf16[32,7168]{1,0:T(8,128)(2,1)S(1)} %get-tuple-element.32), channel_id=1, source_target_pairs={{0,4},{1,13},{2,6},{3,15},{4,8},{5,1},{6,10},{7,3},{8,12},{9,5},{1... | collective-permute-start | bytes 1376264 | tf_op jit(solution)/shard_map/ppermute | solution.py:43
  44.5 1.3 %collective-permute-start.27 = (bf16[8,7168]{1,0:T(8,128)(2,1)S(1)}, bf16[8,7168]{1,0:T(8,128)(2,1)S(1)}, u32[]{:S(2)}, u32[]{:S(2)}) collective-permute-start(bf16[8,7168]{1,0:T(8,128)(2,1)S(1)} %reduce-precision_convert_fusion), channel_id=1, source_target_pairs={{0,128},{16,144},{32,160},{48,176},{64,192},{80,208},{96,224},{112... | collective-permute-start | bytes 344072 | tf_op jit(solution)/shard_map/ppermute | solution.py:43
  45.8 0.5 collective-permute-start.13
  46.3 3.6 %collective-permute-done.5 = bf16[32,7168]{1,0:T(8,128)(2,1)S(1)} collective-permute-done((bf16[32,7168]{1,0:T(8,128)(2,1)S(1)}, bf16[32,7168]{1,0:T(8,128)(2,1)S(1)}, u32[]{:S(2)}, u32[]{:S(2)}) %collective-permute-start.5) | collective-permute-done | bytes 458784 | tf_op jit(solution)/shard_map/ppermute | solution.py:43
  49.9 3.3 %collective-permute-start.2 = (bf16[32,7168]{1,0:T(8,128)(2,1)S(1)}, bf16[32,7168]{1,0:T(8,128)(2,1)S(1)}, u32[]{:S(2)}, u32[]{:S(2)}) collective-permute-start(bf16[32,7168]{1,0:T(8,128)(2,1)S(1)} %get-tuple-element.28), channel_id=1, source_target_pairs={{0,4},{1,13},{2,6},{3,15},{4,8},{5,1},{6,10},{7,3},{8,12},{9,5},{1... | collective-permute-start | bytes 1376264 | tf_op jit(solution)/shard_map/ppermute | solution.py:43
  53.1 0.1 add_convert_fusion.2
  53.4 3.7 %collective-permute-start.20 = (bf16[32,7168]{1,0:T(8,128)(2,1)S(1)}, bf16[32,7168]{1,0:T(8,128)(2,1)S(1)}, u32[]{:S(2)}, u32[]{:S(2)}) collective-permute-start(bf16[32,7168]{1,0:T(8,128)(2,1)S(1)} %collective-permute-done.12.rest_4_), channel_id=1, source_target_pairs={{0,1},{1,0},{2,3},{3,2},{4,5},{5,4},{6,7},{7,6},{8,9},{9,8},{10,11... | collective-permute-start | bytes 1376264 | tf_op jit(solution)/shard_map/ppermute | solution.py:43
  57.1 0.3 collective-permute-start.11
  57.4 1.2 collective-permute-start.7
  58.5 3.0 %collective-permute-done.2 = bf16[32,7168]{1,0:T(8,128)(2,1)S(1)} collective-permute-done((bf16[32,7168]{1,0:T(8,128)(2,1)S(1)}, bf16[32,7168]{1,0:T(8,128)(2,1)S(1)}, u32[]{:S(2)}, u32[]{:S(2)}) %collective-permute-start.2) | collective-permute-done | bytes 458784 | tf_op jit(solution)/shard_map/ppermute | solution.py:43
  61.6 3.4 %collective-permute-start.6 = (bf16[32,7168]{1,0:T(8,128)(2,1)S(1)}, bf16[32,7168]{1,0:T(8,128)(2,1)S(1)}, u32[]{:S(2)}, u32[]{:S(2)}) collective-permute-start(bf16[32,7168]{1,0:T(8,128)(2,1)S(1)} %add_convert_fusion.2), channel_id=1, source_target_pairs={{0,4},{1,13},{2,6},{3,15},{4,8},{5,1},{6,10},{7,3},{8,12},{9,5},{1... | collective-permute-start | bytes 1376264 | tf_op jit(solution)/shard_map/ppermute | solution.py:43
  65.0 0.1 add_convert_fusion.3
  65.1 2.0 %collective-permute-done.14.rest_6_ = bf16[32,7168]{1,0:T(8,128)(2,1)S(1)} collective-permute-done((bf16[32,7168]{1,0:T(8,128)(2,1)S(1)}, bf16[32,7168]{1,0:T(8,128)(2,1)S(1)}, u32[]{:S(2)}, u32[]{:S(2)}) %collective-permute-start.14) | collective-permute-done | bytes 458784 | tf_op jit(solution)/shard_map/ppermute | solution.py:43
  67.1 5.4 %collective-permute-start.17 = (bf16[32,7168]{1,0:T(8,128)(2,1)S(1)}, bf16[32,7168]{1,0:T(8,128)(2,1)S(1)}, u32[]{:S(2)}, u32[]{:S(2)}) collective-permute-start(bf16[32,7168]{1,0:T(8,128)(2,1)S(1)} %collective-permute-done.9.rest_1_), channel_id=1, source_target_pairs={{0,1},{1,0},{2,3},{3,2},{4,5},{5,4},{6,7},{7,6},{8,9},{9,8},{10,11... | collective-permute-start | bytes 1376264 | tf_op jit(solution)/shard_map/ppermute | solution.py:43
  72.5 5.7 %collective-permute-start.18 = (bf16[32,7168]{1,0:T(8,128)(2,1)S(1)}, bf16[32,7168]{1,0:T(8,128)(2,1)S(1)}, u32[]{:S(2)}, u32[]{:S(2)}) collective-permute-start(bf16[32,7168]{1,0:T(8,128)(2,1)S(1)} %collective-permute-done.10.rest_2_), channel_id=1, source_target_pairs={{0,1},{1,0},{2,3},{3,2},{4,5},{5,4},{6,7},{7,6},{8,9},{9,8},{10,11... | collective-permute-start | bytes 1376264 | tf_op jit(solution)/shard_map/ppermute | solution.py:43
  78.2 1.5 %collective-permute-start.15 = (bf16[32,7168]{1,0:T(8,128)(2,1)S(1)}, bf16[32,7168]{1,0:T(8,128)(2,1)S(1)}, u32[]{:S(2)}, u32[]{:S(2)}) collective-permute-start(bf16[32,7168]{1,0:T(8,128)(2,1)S(1)} %collective-permute-done.13.rest_5_), channel_id=1, source_target_pairs={{0,4},{1,13},{2,6},{3,15},{4,8},{5,1},{6,10},{7,3},{8,12},{9,5},{1... | collective-permute-start | bytes 1376264 | tf_op jit(solution)/shard_map/ppermute | solution.py:43
  79.8 3.4 %collective-permute-start.22 = (bf16[32,7168]{1,0:T(8,128)(2,1)S(1)}, bf16[32,7168]{1,0:T(8,128)(2,1)S(1)}, u32[]{:S(2)}, u32[]{:S(2)}) collective-permute-start(bf16[32,7168]{1,0:T(8,128)(2,1)S(1)} %collective-permute-done.14.rest_6_), channel_id=1, source_target_pairs={{0,1},{1,0},{2,3},{3,2},{4,5},{5,4},{6,7},{7,6},{8,9},{9,8},{10,11... | collective-permute-start | bytes 1376264 | tf_op jit(solution)/shard_map/ppermute | solution.py:43
  83.1 0.2 add_convert_fusion.1
  83.3 0.1 collective-permute-start.19
  83.4 2.4 %collective-permute-done.15.rest_7_ = bf16[32,7168]{1,0:T(8,128)(2,1)S(1)} collective-permute-done((bf16[32,7168]{1,0:T(8,128)(2,1)S(1)}, bf16[32,7168]{1,0:T(8,128)(2,1)S(1)}, u32[]{:S(2)}, u32[]{:S(2)}) %collective-permute-start.15) | collective-permute-done | bytes 458784 | tf_op jit(solution)/shard_map/ppermute | solution.py:43
  85.8 2.2 %collective-permute-start.23 = (bf16[32,7168]{1,0:T(8,128)(2,1)S(1)}, bf16[32,7168]{1,0:T(8,128)(2,1)S(1)}, u32[]{:S(2)}, u32[]{:S(2)}) collective-permute-start(bf16[32,7168]{1,0:T(8,128)(2,1)S(1)} %collective-permute-done.15.rest_7_), channel_id=1, source_target_pairs={{0,1},{1,0},{2,3},{3,2},{4,5},{5,4},{6,7},{7,6},{8,9},{9,8},{10,11... | collective-permute-start | bytes 1376264 | tf_op jit(solution)/shard_map/ppermute | solution.py:43
  88.0 0.1 collective-permute-start.4
  88.1 2.6 %collective-permute-start.3 = (bf16[32,7168]{1,0:T(8,128)(2,1)S(1)}, bf16[32,7168]{1,0:T(8,128)(2,1)S(1)}, u32[]{:S(2)}, u32[]{:S(2)}) collective-permute-start(bf16[32,7168]{1,0:T(8,128)(2,1)S(1)} %add_convert_fusion.3), channel_id=1, source_target_pairs={{0,4},{1,13},{2,6},{3,15},{4,8},{5,1},{6,10},{7,3},{8,12},{9,5},{1... | collective-permute-start | bytes 1376264 | tf_op jit(solution)/shard_map/ppermute | solution.py:43
  90.8 0.9 bitcast_subtract_fusion
  91.7 8.7 %weight_and_context_grads.1 = (bf16[256,7168]{1,0:T(8,128)(2,1)}, bf16[512,256]{1,0:T(8,128)(2,1)S(1)}) custom-call(s32[16]{0:T(128)S(1)} %stack.103.at_ref, bf16[512,256]{1,0:T(8,128)(2,1)S(1)} %get-tuple-element.34.ctx_ref, bf16[256,7168]{1,0:T(8,128)(2,1)S(1)} %bitcast.57, bf16[32,7168]{1,0:T(8,128)(2,1)S(1)} %bitcast.68, ...), custom_call_target="tpu_custom_call" | custom-call | flops 3758096384 | bytes 15728640 | tf_op jit(solution)/shard_map/weight_and_context_grads/pallas_call | solution.py:158
  100.4 3.9 %attention_backward.1 = (bf16[512,256]{1,0:T(8,128)(2,1)}, bf16[512,256]{1,0:T(8,128)(2,1)}, bf16[512,256]{1,0:T(8,128)(2,1)}) custom-call(bf16[512,256]{1,0:T(8,128)(2,1)S(1)} %bitcast.59, bf16[512,256]{1,0:T(8,128)(2,1)S(1)} %bitcast.61, bf16[512,256]{1,0:T(8,128)(2,1)S(1)} %bitcast.63, bf16[512,256]{1,0:T(8,128)(2,1)S(1)} %get-tuple-element.36.cg_ref, ...), custom_call_target="tpu_custom_call" | custom-call | flops 536870912 | bytes 4194304 | tf_op jit(solution)/shard_map/attention_backward/pallas_call | solution.py:204
  104.3 11.2 %collective-permute-done.8 = bf16[32,7168]{1,0:T(8,128)(2,1)S(1)} collective-permute-done((bf16[32,7168]{1,0:T(8,128)(2,1)S(1)}, bf16[32,7168]{1,0:T(8,128)(2,1)S(1)}, u32[]{:S(2)}, u32[]{:S(2)}) %collective-permute-start.8) | collective-permute-done | bytes 458784 | tf_op jit(solution)/shard_map/ppermute | solution.py:43
  115.4 1.0 fusion
  (45 shorter events, 0.3 us)
Async XLA Ops:
  0.6 30.9 %collective-permute-start.1 = (bf16[256,7168]{1,0:T(8,128)(2,1)}, bf16[256,7168]{1,0:T(8,128)(2,1)}, u32[]{:S(2)}, u32[]{:S(2)}) collective-permute-start(bf16[256,7168]{1,0:T(8,128)(2,1)} %bitcast.55), channel_id=1, source_target_pairs={{0,1},{1,0},{2,3},{3,2},{4,5},{5,4},{6,7},{7,6},{8,9},{9,8},{10,11... | collective-permute-start | bytes 11010056 | tf_op jit(solution)/shard_map/ppermute | solution.py:43
  5.5 4.8 %collective-permute-start.24 = (bf16[8,7168]{1,0:T(8,128)(2,1)S(1)}, bf16[8,7168]{1,0:T(8,128)(2,1)S(1)}, u32[]{:S(2)}, u32[]{:S(2)}) collective-permute-start(bf16[8,7168]{1,0:T(8,128)(2,1)S(1)} %dynamic-slice_bitcast_fusion), channel_id=1, source_target_pairs={{0,16},{16,0},{32,48},{48,32},{64,80},{80,64},{96,112},{112,96},{1... | collective-permute-start | bytes 344072 | tf_op jit(solution)/shard_map/ppermute | solution.py:43
  11.2 17.0 %collective-permute-start.25 = (bf16[8,7168]{1,0:T(8,128)(2,1)S(1)}, bf16[8,7168]{1,0:T(8,128)(2,1)S(1)}, u32[]{:S(2)}, u32[]{:S(2)}) collective-permute-start(bf16[8,7168]{1,0:T(8,128)(2,1)S(1)} %reduce-precision_convert_fusion.2), channel_id=1, source_target_pairs={{0,32},{16,48},{32,0},{48,16},{64,96},{80,112},{96,64},{112,80},{1... | collective-permute-start | bytes 344072 | tf_op jit(solution)/shard_map/ppermute | solution.py:43
  12.3 32.2 %collective-permute-start.12 = (bf16[32,7168]{1,0:T(8,128)(2,1)}, bf16[32,7168]{1,0:T(8,128)(2,1)S(1)}, u32[]{:S(2)}, u32[]{:S(2)}) collective-permute-start(bf16[32,7168]{1,0:T(8,128)(2,1)} %bitcast.64), channel_id=1, source_target_pairs={{0,2},{1,3},{2,0},{3,1},{4,6},{5,7},{6,4},{7,5},{8,10},{9,11},{10,... | collective-permute-start | bytes 1376264 | tf_op jit(solution)/shard_map/ppermute | solution.py:43
  19.2 26.6 %collective-permute-start.9 = (bf16[32,7168]{1,0:T(8,128)(2,1)}, bf16[32,7168]{1,0:T(8,128)(2,1)S(1)}, u32[]{:S(2)}, u32[]{:S(2)}) collective-permute-start(bf16[32,7168]{1,0:T(8,128)(2,1)} %bitcast.65), channel_id=1, source_target_pairs={{0,4},{1,13},{2,6},{3,15},{4,8},{5,1},{6,10},{7,3},{8,12},{9,5},{1... | collective-permute-start | bytes 1376264 | tf_op jit(solution)/shard_map/ppermute | solution.py:43
  22.0 31.3 %collective-permute-start.10 = (bf16[32,7168]{1,0:T(8,128)(2,1)}, bf16[32,7168]{1,0:T(8,128)(2,1)S(1)}, u32[]{:S(2)}, u32[]{:S(2)}) collective-permute-start(bf16[32,7168]{1,0:T(8,128)(2,1)} %bitcast.66), channel_id=1, source_target_pairs={{0,12},{1,5},{2,14},{3,7},{4,0},{5,9},{6,2},{7,11},{8,4},{9,13},{1... | collective-permute-start | bytes 1376264 | tf_op jit(solution)/shard_map/ppermute | solution.py:43
  22.2 1.0 copy-start.2
  23.1 0.9 copy-start.4
  24.1 0.9 copy-start.6
  28.2 2.9 %collective-permute-start = (bf16[256,256]{1,0:T(8,128)(2,1)S(1)}, bf16[256,256]{1,0:T(8,128)(2,1)S(1)}, u32[]{:S(2)}, u32[]{:S(2)}) collective-permute-start(bf16[256,256]{1,0:T(8,128)(2,1)S(1)} %get-tuple-element.25), channel_id=1, source_target_pairs={{0,1},{1,0},{2,3},{3,2},{4,5},{5,4},{6,7},{7,6},{8,9},{9,8},{10,11... | collective-permute-start | bytes 393224 | tf_op jit(solution)/shard_map/ppermute | solution.py:43
  31.2 22.2 %collective-permute-start.16 = (bf16[32,7168]{1,0:T(8,128)(2,1)}, bf16[32,7168]{1,0:T(8,128)(2,1)S(1)}, u32[]{:S(2)}, u32[]{:S(2)}) collective-permute-start(bf16[32,7168]{1,0:T(8,128)(2,1)} %bitcast.67), channel_id=1, source_target_pairs={{0,1},{1,0},{2,3},{3,2},{4,5},{5,4},{6,7},{7,6},{8,9},{9,8},{10,11... | collective-permute-start | bytes 1376264 | tf_op jit(solution)/shard_map/ppermute | solution.py:43
  31.5 10.2 %collective-permute-start.26 = (bf16[8,7168]{1,0:T(8,128)(2,1)S(1)}, bf16[8,7168]{1,0:T(8,128)(2,1)S(1)}, u32[]{:S(2)}, u32[]{:S(2)}) collective-permute-start(bf16[8,7168]{1,0:T(8,128)(2,1)S(1)} %reduce-precision_convert_fusion.1), channel_id=1, source_target_pairs={{0,64},{16,80},{32,96},{48,112},{64,0},{80,16},{96,32},{112,48},{1... | collective-permute-start | bytes 344072 | tf_op jit(solution)/shard_map/ppermute | solution.py:43
  32.3 2.0 %copy-start = (bf16[1,256,7168]{2,1,0:T(8,128)(2,1)S(1)}, bf16[1,256,7168]{2,1,0:T(8,128)(2,1)}, u32[]{:S(2)}) copy-start(bf16[1,256,7168]{2,1,0:T(8,128)(2,1)} %param.12) | copy-start | bytes 11010052
  34.3 56.4 %copy-start.10 = (f32[2,8,7168]{2,1,0:T(8,128)S(1)}, f32[2,8,7168]{2,1,0:T(8,128)}, u32[]{:S(2)}) copy-start(f32[2,8,7168]{2,1,0:T(8,128)} %param.16) | copy-start | bytes 1376260
  40.9 49.8 %copy-start.9 = (f32[2,8,7168]{2,1,0:T(8,128)S(1)}, f32[2,8,7168]{2,1,0:T(8,128)}, u32[]{:S(2)}) copy-start(f32[2,8,7168]{2,1,0:T(8,128)} %param.15) | copy-start | bytes 1376260
  40.9 50.7 %copy-start.1 = (bf16[1,256,7168]{2,1,0:T(8,128)(2,1)S(1)}, bf16[1,256,7168]{2,1,0:T(8,128)(2,1)}, u32[]{:S(2)}) copy-start(bf16[1,256,7168]{2,1,0:T(8,128)(2,1)} %param.12) | copy-start | bytes 11010052
  40.9 50.7 %copy-start.8 = (bf16[1,32,7168]{2,1,0:T(8,128)(2,1)S(1)}, bf16[1,32,7168]{2,1,0:T(8,128)(2,1)}, u32[]{:S(2)}) copy-start(bf16[1,32,7168]{2,1,0:T(8,128)(2,1)} %param.13) | copy-start | bytes 1376260
  41.7 8.2 %collective-permute-start.5 = (bf16[32,7168]{1,0:T(8,128)(2,1)S(1)}, bf16[32,7168]{1,0:T(8,128)(2,1)S(1)}, u32[]{:S(2)}, u32[]{:S(2)}) collective-permute-start(bf16[32,7168]{1,0:T(8,128)(2,1)S(1)} %get-tuple-element.32), channel_id=1, source_target_pairs={{0,4},{1,13},{2,6},{3,15},{4,8},{5,1},{6,10},{7,3},{8,12},{9,5},{1... | collective-permute-start | bytes 1376264 | tf_op jit(solution)/shard_map/ppermute | solution.py:43
  44.5 12.6 %collective-permute-start.27 = (bf16[8,7168]{1,0:T(8,128)(2,1)S(1)}, bf16[8,7168]{1,0:T(8,128)(2,1)S(1)}, u32[]{:S(2)}, u32[]{:S(2)}) collective-permute-start(bf16[8,7168]{1,0:T(8,128)(2,1)S(1)} %reduce-precision_convert_fusion), channel_id=1, source_target_pairs={{0,128},{16,144},{32,160},{48,176},{64,192},{80,208},{96,224},{112... | collective-permute-start | bytes 344072 | tf_op jit(solution)/shard_map/ppermute | solution.py:43
  45.8 11.6 %collective-permute-start.13 = (bf16[32,7168]{1,0:T(8,128)(2,1)S(1)}, bf16[32,7168]{1,0:T(8,128)(2,1)S(1)}, u32[]{:S(2)}, u32[]{:S(2)}) collective-permute-start(bf16[32,7168]{1,0:T(8,128)(2,1)S(1)} %collective-permute-done.12.rest_4_), channel_id=1, source_target_pairs={{0,4},{1,13},{2,6},{3,15},{4,8},{5,1},{6,10},{7,3},{8,12},{9,5},{1... | collective-permute-start | bytes 1376264 | tf_op jit(solution)/shard_map/ppermute | solution.py:43
  49.9 11.7 %collective-permute-start.2 = (bf16[32,7168]{1,0:T(8,128)(2,1)S(1)}, bf16[32,7168]{1,0:T(8,128)(2,1)S(1)}, u32[]{:S(2)}, u32[]{:S(2)}) collective-permute-start(bf16[32,7168]{1,0:T(8,128)(2,1)S(1)} %get-tuple-element.28), channel_id=1, source_target_pairs={{0,4},{1,13},{2,6},{3,15},{4,8},{5,1},{6,10},{7,3},{8,12},{9,5},{1... | collective-permute-start | bytes 1376264 | tf_op jit(solution)/shard_map/ppermute | solution.py:43
  53.3 13.9 %collective-permute-start.14 = (bf16[32,7168]{1,0:T(8,128)(2,1)S(1)}, bf16[32,7168]{1,0:T(8,128)(2,1)S(1)}, u32[]{:S(2)}, u32[]{:S(2)}) collective-permute-start(bf16[32,7168]{1,0:T(8,128)(2,1)S(1)} %collective-permute-done.12.rest_4_), channel_id=1, source_target_pairs={{0,12},{1,5},{2,14},{3,7},{4,0},{5,9},{6,2},{7,11},{8,4},{9,13},{1... | collective-permute-start | bytes 1376264 | tf_op jit(solution)/shard_map/ppermute | solution.py:43
  53.4 24.9 %collective-permute-start.20 = (bf16[32,7168]{1,0:T(8,128)(2,1)S(1)}, bf16[32,7168]{1,0:T(8,128)(2,1)S(1)}, u32[]{:S(2)}, u32[]{:S(2)}) collective-permute-start(bf16[32,7168]{1,0:T(8,128)(2,1)S(1)} %collective-permute-done.12.rest_4_), channel_id=1, source_target_pairs={{0,1},{1,0},{2,3},{3,2},{4,5},{5,4},{6,7},{7,6},{8,9},{9,8},{10,11... | collective-permute-start | bytes 1376264 | tf_op jit(solution)/shard_map/ppermute | solution.py:43
  57.1 15.4 %collective-permute-start.11 = (bf16[32,7168]{1,0:T(8,128)(2,1)S(1)}, bf16[32,7168]{1,0:T(8,128)(2,1)S(1)}, u32[]{:S(2)}, u32[]{:S(2)}) collective-permute-start(bf16[32,7168]{1,0:T(8,128)(2,1)S(1)} %collective-permute-done.9.rest_1_), channel_id=1, source_target_pairs={{0,4},{1,13},{2,6},{3,15},{4,8},{5,1},{6,10},{7,3},{8,12},{9,5},{1... | collective-permute-start | bytes 1376264 | tf_op jit(solution)/shard_map/ppermute | solution.py:43
  57.4 22.3 %collective-permute-start.7 = (bf16[32,7168]{1,0:T(8,128)(2,1)S(1)}, bf16[32,7168]{1,0:T(8,128)(2,1)S(1)}, u32[]{:S(2)}, u32[]{:S(2)}) collective-permute-start(bf16[32,7168]{1,0:T(8,128)(2,1)S(1)} %get-tuple-element.33), channel_id=1, source_target_pairs={{0,12},{1,5},{2,14},{3,7},{4,0},{5,9},{6,2},{7,11},{8,4},{9,13},{1... | collective-permute-start | bytes 1376264 | tf_op jit(solution)/shard_map/ppermute | solution.py:43
  61.6 18.2 %collective-permute-start.6 = (bf16[32,7168]{1,0:T(8,128)(2,1)S(1)}, bf16[32,7168]{1,0:T(8,128)(2,1)S(1)}, u32[]{:S(2)}, u32[]{:S(2)}) collective-permute-start(bf16[32,7168]{1,0:T(8,128)(2,1)S(1)} %add_convert_fusion.2), channel_id=1, source_target_pairs={{0,4},{1,13},{2,6},{3,15},{4,8},{5,1},{6,10},{7,3},{8,12},{9,5},{1... | collective-permute-start | bytes 1376264 | tf_op jit(solution)/shard_map/ppermute | solution.py:43
  67.1 16.2 %collective-permute-start.17 = (bf16[32,7168]{1,0:T(8,128)(2,1)S(1)}, bf16[32,7168]{1,0:T(8,128)(2,1)S(1)}, u32[]{:S(2)}, u32[]{:S(2)}) collective-permute-start(bf16[32,7168]{1,0:T(8,128)(2,1)S(1)} %collective-permute-done.9.rest_1_), channel_id=1, source_target_pairs={{0,1},{1,0},{2,3},{3,2},{4,5},{5,4},{6,7},{7,6},{8,9},{9,8},{10,11... | collective-permute-start | bytes 1376264 | tf_op jit(solution)/shard_map/ppermute | solution.py:43
  72.5 15.5 %collective-permute-start.18 = (bf16[32,7168]{1,0:T(8,128)(2,1)S(1)}, bf16[32,7168]{1,0:T(8,128)(2,1)S(1)}, u32[]{:S(2)}, u32[]{:S(2)}) collective-permute-start(bf16[32,7168]{1,0:T(8,128)(2,1)S(1)} %collective-permute-done.10.rest_2_), channel_id=1, source_target_pairs={{0,1},{1,0},{2,3},{3,2},{4,5},{5,4},{6,7},{7,6},{8,9},{9,8},{10,11... | collective-permute-start | bytes 1376264 | tf_op jit(solution)/shard_map/ppermute | solution.py:43
  78.2 7.6 %collective-permute-start.15 = (bf16[32,7168]{1,0:T(8,128)(2,1)S(1)}, bf16[32,7168]{1,0:T(8,128)(2,1)S(1)}, u32[]{:S(2)}, u32[]{:S(2)}) collective-permute-start(bf16[32,7168]{1,0:T(8,128)(2,1)S(1)} %collective-permute-done.13.rest_5_), channel_id=1, source_target_pairs={{0,4},{1,13},{2,6},{3,15},{4,8},{5,1},{6,10},{7,3},{8,12},{9,5},{1... | collective-permute-start | bytes 1376264 | tf_op jit(solution)/shard_map/ppermute | solution.py:43
  79.7 8.4 %collective-permute-start.21 = (bf16[32,7168]{1,0:T(8,128)(2,1)S(1)}, bf16[32,7168]{1,0:T(8,128)(2,1)S(1)}, u32[]{:S(2)}, u32[]{:S(2)}) collective-permute-start(bf16[32,7168]{1,0:T(8,128)(2,1)S(1)} %collective-permute-done.13.rest_5_), channel_id=1, source_target_pairs={{0,1},{1,0},{2,3},{3,2},{4,5},{5,4},{6,7},{7,6},{8,9},{9,8},{10,11... | collective-permute-start | bytes 1376264 | tf_op jit(solution)/shard_map/ppermute | solution.py:43
  79.8 11.0 %collective-permute-start.22 = (bf16[32,7168]{1,0:T(8,128)(2,1)S(1)}, bf16[32,7168]{1,0:T(8,128)(2,1)S(1)}, u32[]{:S(2)}, u32[]{:S(2)}) collective-permute-start(bf16[32,7168]{1,0:T(8,128)(2,1)S(1)} %collective-permute-done.14.rest_6_), channel_id=1, source_target_pairs={{0,1},{1,0},{2,3},{3,2},{4,5},{5,4},{6,7},{7,6},{8,9},{9,8},{10,11... | collective-permute-start | bytes 1376264 | tf_op jit(solution)/shard_map/ppermute | solution.py:43
  83.3 8.3 %collective-permute-start.19 = (bf16[32,7168]{1,0:T(8,128)(2,1)S(1)}, bf16[32,7168]{1,0:T(8,128)(2,1)S(1)}, u32[]{:S(2)}, u32[]{:S(2)}) collective-permute-start(bf16[32,7168]{1,0:T(8,128)(2,1)S(1)} %collective-permute-done.11.rest_3_), channel_id=1, source_target_pairs={{0,1},{1,0},{2,3},{3,2},{4,5},{5,4},{6,7},{7,6},{8,9},{9,8},{10,11... | collective-permute-start | bytes 1376264 | tf_op jit(solution)/shard_map/ppermute | solution.py:43
  85.8 5.8 %collective-permute-start.23 = (bf16[32,7168]{1,0:T(8,128)(2,1)S(1)}, bf16[32,7168]{1,0:T(8,128)(2,1)S(1)}, u32[]{:S(2)}, u32[]{:S(2)}) collective-permute-start(bf16[32,7168]{1,0:T(8,128)(2,1)S(1)} %collective-permute-done.15.rest_7_), channel_id=1, source_target_pairs={{0,1},{1,0},{2,3},{3,2},{4,5},{5,4},{6,7},{7,6},{8,9},{9,8},{10,11... | collective-permute-start | bytes 1376264 | tf_op jit(solution)/shard_map/ppermute | solution.py:43
  88.0 16.2 %collective-permute-start.4 = (bf16[32,7168]{1,0:T(8,128)(2,1)S(1)}, bf16[32,7168]{1,0:T(8,128)(2,1)S(1)}, u32[]{:S(2)}, u32[]{:S(2)}) collective-permute-start(bf16[32,7168]{1,0:T(8,128)(2,1)S(1)} %get-tuple-element.29), channel_id=1, source_target_pairs={{0,12},{1,5},{2,14},{3,7},{4,0},{5,9},{6,2},{7,11},{8,4},{9,13},{1... | collective-permute-start | bytes 1376264 | tf_op jit(solution)/shard_map/ppermute | solution.py:43
  88.1 16.1 %collective-permute-start.3 = (bf16[32,7168]{1,0:T(8,128)(2,1)S(1)}, bf16[32,7168]{1,0:T(8,128)(2,1)S(1)}, u32[]{:S(2)}, u32[]{:S(2)}) collective-permute-start(bf16[32,7168]{1,0:T(8,128)(2,1)S(1)} %add_convert_fusion.3), channel_id=1, source_target_pairs={{0,4},{1,13},{2,6},{3,15},{4,8},{5,1},{6,10},{7,3},{8,12},{9,5},{1... | collective-permute-start | bytes 1376264 | tf_op jit(solution)/shard_map/ppermute | solution.py:43
  90.7 24.7 %collective-permute-start.8 = (bf16[32,7168]{1,0:T(8,128)(2,1)S(1)}, bf16[32,7168]{1,0:T(8,128)(2,1)S(1)}, u32[]{:S(2)}, u32[]{:S(2)}) collective-permute-start(bf16[32,7168]{1,0:T(8,128)(2,1)S(1)} %add_convert_fusion.1), channel_id=1, source_target_pairs={{0,2},{1,3},{2,0},{3,1},{4,6},{5,7},{6,4},{7,5},{8,10},{9,11},{10,... | collective-permute-start | bytes 1376264 | tf_op jit(solution)/shard_map/ppermute | solution.py:43
  91.6 8.8 %copy-start.3 = (bf16[1,512,256]{2,1,0:T(8,128)(2,1)S(1)}, bf16[1,512,256]{2,1,0:T(8,128)(2,1)}, u32[]{:S(2)}) copy-start(bf16[1,512,256]{2,1,0:T(8,128)(2,1)} %param.9) | copy-start | bytes 786436
  91.6 8.8 %copy-start.5 = (bf16[1,512,256]{2,1,0:T(8,128)(2,1)S(1)}, bf16[1,512,256]{2,1,0:T(8,128)(2,1)}, u32[]{:S(2)}) copy-start(bf16[1,512,256]{2,1,0:T(8,128)(2,1)} %param.10) | copy-start | bytes 786436
  91.7 8.7 %copy-start.7 = (bf16[1,512,256]{2,1,0:T(8,128)(2,1)S(1)}, bf16[1,512,256]{2,1,0:T(8,128)(2,1)}, u32[]{:S(2)}) copy-start(bf16[1,512,256]{2,1,0:T(8,128)(2,1)} %param.11) | copy-start | bytes 786436

commit v2 on v1

v2 whole, which is shorter than its diff:
```python
import functools

import jax
import jax.numpy as jnp
from jax import lax
from jax.experimental import pallas as pl
from jax.experimental.pallas import tpu as pltpu
from jax.sharding import PartitionSpec as P

HD = 128
ROWS = 256
N_Y = 4
F32 = jnp.float32
BF16 = jnp.bfloat16

outer_momentum = 0.9
outer_rate = 0.7
SMEM = pltpu.SMEM
VMEM = 24 << 20


def tp_index(y, z, c):
    return (y % N_Y) * 4 + z * 2 + c


def tp_moves(move):
    return [
        (tp_index(y, z, c), tp_index(*move(y, z, c)))
        for y in range(N_Y)
        for z in range(2)
        for c in range(2)
    ]


AHEAD = tp_moves(lambda y, z, c: (y + 1 - 2 * c, z, c))
BACK = tp_moves(lambda y, z, c: (y - 1 + 2 * c, z, c))
ACROSS = tp_moves(lambda y, z, c: (y, 1 - z, c))
OTHER_CORE = tp_moves(lambda y, z, c: (y, z, 1 - c))
REP_STEPS = [[(r, r ^ bit) for r in range(16)] for bit in (1, 2, 4, 8)]


def send(value, moves, axis="tp"):
    return lax.ppermute(value, axis, moves)


def softmax_rows(q, k, first):
    rows, seen = q.shape[0], k.shape[0]
    scores = lax.dot_general(q, k, (((1,), (1,)), ((), ())), preferred_element_type=F32)
    row = lax.broadcasted_iota(jnp.int32, (rows, seen), 0) + first
    col = lax.broadcasted_iota(jnp.int32, (rows, seen), 1)
    scores = jnp.where(row >= col, scores * HD ** (-0.5), -1e30)
    weights = jnp.exp(scores - jnp.max(scores, axis=-1, keepdims=True))
    return weights * (1.0 / jnp.sum(weights, axis=-1, keepdims=True))


def forward_kernel(core_ref, q_ref, k_ref, v_ref, ctx_ref, keep_ref, give_ref):
    core = core_ref[0]
    tokens, cols = q_ref.shape
    for h in range(cols // HD):
        head = pl.ds(h * HD, HD)
        for i in range(tokens // ROWS):
            seen, mine = pl.ds(0, ROWS * (i + 1)), pl.ds(i * ROWS, ROWS)
            probs = softmax_rows(q_ref[mine, head], k_ref[seen, head], i * ROWS)
            ctx = jnp.dot(probs.astype(BF16), v_ref[seen, head], preferred_element_type=F32).astype(BF16)
            ctx_ref[mine, head] = ctx
            even = jnp.concatenate([ctx[r : r + 32] for r in range(0, ROWS, 64)], axis=0)
            odd = jnp.concatenate([ctx[r + 32 : r + 64] for r in range(0, ROWS, 64)], axis=0)
            half = pl.ds(i * (ROWS // 2), ROWS // 2)
            keep_ref[half, head] = jnp.where(core == 0, even, odd)
            give_ref[half, head] = jnp.where(core == 0, odd, even)


def attention_forward(core, q, k, v):
    tokens, cols = q.shape
    vmem = pl.BlockSpec(memory_space=pltpu.VMEM)
    return pl.pallas_call(
        forward_kernel,
        in_specs=[pl.BlockSpec(memory_space=SMEM), vmem, vmem, vmem],
        out_specs=[vmem] * 3,
        out_shape=[
            jax.ShapeDtypeStruct((tokens, cols), BF16),
            jax.ShapeDtypeStruct((tokens // 2, cols), BF16),
            jax.ShapeDtypeStruct((tokens // 2, cols), BF16),
        ],
        compiler_params=pltpu.CompilerParams(vmem_limit_bytes=VMEM),
                name="attention_forward",
    )(core, q, k, v)


def project_kernel(at_ref, mine_ref, theirs_ref, w_ref, w2_ref, *rest):
    outs, held = rest[:-1], rest[-1]
    part = jnp.dot(mine_ref[...], w_ref[...], preferred_element_type=F32)
    part += jnp.dot(theirs_ref[...], w2_ref[...], preferred_element_type=F32)
    held[...] = part.astype(BF16)
    for i, out in enumerate(outs):
        out[...] = held[pl.ds(pl.multiple_of(at_ref[i], 32), 32), :]


def project(at, mine, theirs, w, w2, blk=3584):
    rows, cols = mine.shape
    width = w.shape[1]
    whole = pl.BlockSpec((rows, cols), lambda j: (0, 0))
    weight = pl.BlockSpec((cols, blk), lambda j: (0, j))
    chunk = pl.BlockSpec((32, blk), lambda j: (0, j))
    n = rows // 32
    return pl.pallas_call(
        project_kernel,
        grid=(width // blk,),
        in_specs=[pl.BlockSpec(memory_space=SMEM), whole, whole, weight, weight],
        out_specs=[chunk] * n,
        out_shape=[jax.ShapeDtypeStruct((32, width), BF16)] * n,
        scratch_shapes=[pltpu.VMEM((rows, blk), BF16)],
        compiler_params=pltpu.CompilerParams(vmem_limit_bytes=VMEM),
                name="project",
    )(at, mine, theirs, w, w2)


def weight_kernel(n, at_ref, ctx_ref, w_ref, *rest):
    pieces, (wg_ref, cg_ref, held, acc, flipped) = rest[:n], rest[n:]
    j = pl.program_id(0)

    @pl.when(j == 0)
    def _():
        flipped[...] = ctx_ref[...].T

    for i, piece in enumerate(pieces):
        held[pl.ds(pl.multiple_of(at_ref[i], 32), 32), :] = piece[...]
    block = held[...]
    wg = jnp.dot(flipped[...], block, preferred_element_type=F32)
    wg_ref[...] = wg.astype(BF16)
    part = lax.dot_general(block, w_ref[...], (((1,), (1,)), ((), ())), preferred_element_type=F32)

    @pl.when(j == 0)
    def _():
        acc[...] = part

    @pl.when(j > 0)
    def _():
        acc[...] += part

    @pl.when(j == pl.num_programs(0) - 1)
    def _():
        cg_ref[...] = acc[...].astype(BF16)


def weight_and_context_grads(at, ctx, w, pieces, blk=1792):
    tokens, cols = ctx.shape
    width = w.shape[1]
    n = len(pieces)
    whole = pl.BlockSpec((tokens, cols), lambda j: (0, 0))
    weight = pl.BlockSpec((cols, blk), lambda j: (0, j))
    chunk = pl.BlockSpec((32, blk), lambda j: (0, j))
    return pl.pallas_call(
        functools.partial(weight_kernel, n),
        grid=(width // blk,),
        in_specs=[pl.BlockSpec(memory_space=SMEM), whole, weight] + [chunk] * n,
        out_specs=[weight, whole],
        out_shape=[jax.ShapeDtypeStruct((cols, width), BF16), jax.ShapeDtypeStruct((tokens, cols), BF16)],
        scratch_shapes=[
            pltpu.VMEM((tokens, blk), BF16),
            pltpu.VMEM((tokens, cols), F32),
            pltpu.VMEM((cols, tokens), BF16),
        ],
        compiler_params=pltpu.CompilerParams(vmem_limit_bytes=VMEM),
                name="weight_and_context_grads",
    )(at, ctx, w, *pieces)


def backward_kernel(q_ref, k_ref, v_ref, cg_ref, dq_ref, dk_ref, dv_ref, dk_acc, dv_acc):
    tokens, cols = q_ref.shape
    blocks = tokens // ROWS
    for h in range(cols // HD):
        head = pl.ds(h * HD, HD)
        for i in reversed(range(blocks)):
            mine, seen = pl.ds(i * ROWS, ROWS), pl.ds(0, ROWS * (i + 1))
            q, k, cg = q_ref[mine, head], k_ref[seen, head], cg_ref[mine, head]
            probs = softmax_rows(q, k, i * ROWS)
            probs_grad = lax.dot_general(
                cg, v_ref[seen, head], (((1,), (1,)), ((), ())), preferred_element_type=F32
            )
            inner = jnp.sum(probs * probs_grad, axis=-1, keepdims=True)
            score_grad = (probs * (probs_grad - inner) * HD ** (-0.5)).astype(BF16)
            dq_ref[mine, head] = jnp.dot(score_grad, k, preferred_element_type=F32).astype(BF16)
            dk = lax.dot_general(score_grad, q, (((0,), (0,)), ((), ())), preferred_element_type=F32)
            dv = lax.dot_general(probs.astype(BF16), cg, (((0,), (0,)), ((), ())), preferred_element_type=F32)
            if i == blocks - 1:
                dk_acc[:, head] = dk
                dv_acc[:, head] = dv
            else:
                dk_acc[seen, head] += dk
                dv_acc[seen, head] += dv
    dk_ref[...] = dk_acc[...].astype(BF16)
    dv_ref[...] = dv_acc[...].astype(BF16)


def attention_backward(q, k, v, cg):
    tokens, cols = q.shape
    vmem = pl.BlockSpec(memory_space=pltpu.VMEM)
    return pl.pallas_call(
        backward_kernel,
        in_specs=[vmem] * 4,
        out_specs=[vmem] * 3,
        out_shape=[jax.ShapeDtypeStruct((tokens, cols), BF16)] * 3,
        scratch_shapes=[pltpu.VMEM((tokens, cols), F32)] * 2,
        compiler_params=pltpu.CompilerParams(vmem_limit_bytes=VMEM),
                name="attention_backward",
    )(q, k, v, cg)


def add(*terms):
    total = terms[0].astype(F32)
    for term in terms[1:]:
        total = total + term.astype(F32)
    return total.astype(BF16)


def nesterov(outer_old, moment_old, summed):
    average = summed / lax.axis_size("rep")
    pseudo_grad = outer_old - average
    new_momentum = outer_momentum * moment_old + pseudo_grad
    new_global = outer_old - outer_rate * (outer_momentum * new_momentum + pseudo_grad)
    return (new_global, new_momentum)


def after(value, *earlier):
    return lax.optimization_barrier((value, *earlier))[0]


class Line:
    def __init__(self):
        self.sent = []

    def send(self, value, moves):
        if len(self.sent) >= 2:
            value = after(value, self.sent[-2])
        self.sent.append(send(value, moves))
        return self.sent[-1]


def shards(
    queries, keys, values, out_weight, cotangent, local_params, global_params, momentum, frag_index
):
    q, k, v, w, x = queries[0], keys[0], values[0], out_weight[0], cotangent[0]
    q, k, v, w = (pltpu.with_memory_space_constraint(a, pltpu.HBM) for a in (q, k, v, w))
    me = lax.axis_index("tp")
    y, z, c = me // 4, (me // 2) % 2, me % 2
    ahead = 1 - 2 * c
    line = Line()

    far = send(x, ACROSS)
    near1 = line.send(x, AHEAD)
    near2 = line.send(x, BACK)
    w2 = send(w, OTHER_CORE)

    core = jnp.reshape(c, (1,)).astype(jnp.int32)
    ctx, keep, give = attention_forward(core, q, k, v)
    theirs = send(give, OTHER_CORE)
    at = [
        ((jnp.mod(y + hop * ahead, N_Y)) * 2 + zz) * 32 for zz in (z, 1 - z) for hop in (0, 1, 2, 3)
    ]
    parts = project(jnp.stack(at).astype(jnp.int32), keep, theirs, w, w2)
    own, other = parts[:4], parts[4:]
    near3 = line.send(after(near1, parts[0]), AHEAD)

    first = line.send(other[2], AHEAD)
    side = line.send(other[3], BACK)
    middle = add(other[1], first)
    second = line.send(middle, AHEAD)
    far1 = line.send(far, AHEAD)
    crossing = add(other[0], second, side)
    crossed = send(crossing, ACROSS)
    far2 = line.send(far, BACK)
    far3 = line.send(far1, AHEAD)

    first2 = line.send(own[2], AHEAD)
    side2 = line.send(own[3], BACK)
    middle2 = add(own[1], first2)
    second2 = line.send(middle2, AHEAD)
    branch_out = add(own[0], second2, side2, crossed)

    mine = [x, near1, near2, near3, far, far1, far2, far3]
    pieces = mine + [send(piece, OTHER_CORE) for piece in mine]
    token_at = [
        (jnp.mod(y + hop * sign, N_Y) * 4 + zz * 2 + cc) * 32
        for cc, sign in ((c, ahead), (1 - c, -ahead))
        for zz in (z, 1 - z)
        for hop in (0, -1, 1, -2)
    ]
    weight_grad, cg = weight_and_context_grads(jnp.stack(token_at).astype(jnp.int32), ctx, w, pieces)
    dq, dk, dv = attention_backward(q, k, v, after(cg, middle2))

    chosen = frag_index[0]
    part = lax.dynamic_index_in_dim(local_params[0], chosen, 0, keepdims=False)
    outer_old = lax.dynamic_index_in_dim(global_params, chosen, 0, keepdims=False)
    moment_old = lax.dynamic_index_in_dim(momentum, chosen, 0, keepdims=False)
    for moves, ready in zip(REP_STEPS, (near3, side, middle, far1)):
        part = after(part, ready)
        total = part.astype(F32) + send(part, moves, "rep").astype(F32)
        part = lax.reduce_precision(total, 8, 7).astype(BF16)
    new_global, new_momentum = nesterov(outer_old, moment_old, total)
    return (branch_out[None], weight_grad[None], dq[None], dk[None], dv[None], new_global, new_momentum)


def solution(mesh):
    placed = (
        P("rep", None, "tp"),
        P("rep", None, "tp"),
        P("rep", None, "tp"),
        P("rep", "tp", None),
        P("rep", "tp", None),
        P("rep", None, "tp", None),
        P(None, "tp", None),
        P(None, "tp", None),
        P(),
    )
    return jax.shard_map(
        shards,
        mesh=mesh,
        in_specs=placed,
        out_specs=(
            P("rep", "tp", None),
            P("rep", "tp", None),
            P("rep", None, "tp"),
            P("rep", None, "tp"),
            P("rep", None, "tp"),
            P("tp", None),
            P("tp", None),
        ),
        check_vma=False,
    )
```

time: 117 us -> 104 us (0.89)
  the two profiles are of different devices: /device:TPU:1 before, /device:TPU:36 now
where the time goes in v2:
time: 104 us
  waiting for transfers between devices  47.9 us (46%)
  starting transfers between devices  22.9 us (22%)
  Pallas kernels  20.4 us (20%)
  other arithmetic  6.86 us (7%)
  local copies, waits for them, and re-layouts  4.3 us (4%)
  between operations  1.52 us (1%)
    ppermute x28, waiting for transfers between devices, send(): return lax.ppermute(value, axis, moves)  47.9 us
    ppermute x28, starting transfers between devices, send(): return lax.ppermute(value, axis, moves)  22.9 us
    pallas_call x1, Pallas kernels, weight_and_context_grads(): pl.pallas_call(functools.partial(weight_kernel, n), grid=(width // blk,),...  7.96 us
    pallas_call x1, Pallas kernels, project(): pl.pallas_call(project_kernel, grid=(width // blk,), in_specs=[pl.BlockSp...  4.94 us
    pallas_call x1, Pallas kernels, attention_backward(): pl.pallas_call(backward_kernel, in_specs=[vmem] * 4, out_specs=[vmem] * 3...  4.57 us
    unnamed x30, local copies, waits for them, and re-layouts  4.11 us
    convert_element_type x3, other arithmetic, add(): return total.astype(BF16)  3.32 us
    pallas_call x1, Pallas kernels, attention_forward(): pl.pallas_call(forward_kernel, in_specs=[pl.BlockSpec(memory_space=SMEM),...  2.9 us
  transfers between devices with their start and end apart: 28, of which 9 were waited for; matrix products, arithmetic and copies ran while one was open for 6% of the time, Pallas kernels for 20%

profile of v2, /device:TPU:36, one launch (start us, length us, event | category | flops | bytes accessed | tf_op | source)
XLA Modules:
  0.0 103.9 jit_solution(7340716072055967403)
XLA Ops:
  0.6 0.0 copy-start
  0.6 0.1 collective-permute-start.1
  0.8 1.7 %collective-permute-start.9 = (bf16[32,7168]{1,0:T(8,128)(2,1)}, bf16[32,7168]{1,0:T(8,128)(2,1)S(1)}, u32[]{:S(2)}, u32[]{:S(2)}) collective-permute-start(bf16[32,7168]{1,0:T(8,128)(2,1)} %bitcast.53), channel_id=1, source_target_pairs={{0,4},{1,13},{2,6},{3,15},{4,8},{5,1},{6,10},{7,3},{8,12},{9,5},{1... | collective-permute-start | bytes 1376264 | tf_op jit(solution)/shard_map/ppermute | solution.py:43
  2.4 1.7 %collective-permute-start.3 = (bf16[32,7168]{1,0:T(8,128)(2,1)}, bf16[32,7168]{1,0:T(8,128)(2,1)S(1)}, u32[]{:S(2)}, u32[]{:S(2)}) collective-permute-start(bf16[32,7168]{1,0:T(8,128)(2,1)} %bitcast.54), channel_id=1, source_target_pairs={{0,12},{1,5},{2,14},{3,7},{4,0},{5,9},{6,2},{7,11},{8,4},{9,13},{1... | collective-permute-start | bytes 1376264 | tf_op jit(solution)/shard_map/ppermute | solution.py:43
  4.1 2.9 %attention_forward.1 = (bf16[512,256]{1,0:T(8,128)(2,1)S(1)}, bf16[256,256]{1,0:T(8,128)(2,1)S(1)}, bf16[256,256]{1,0:T(8,128)(2,1)S(1)}) custom-call(s32[1]{0:T(128)} %bitcast.8.core_ref, bf16[512,256]{1,0:T(8,128)(2,1)} %bitcast.61, bf16[512,256]{1,0:T(8,128)(2,1)} %bitcast.63, bf16[512,256]{1,0:T(8,128)(2,1)} %bitcast.65), custom_call_target="tpu_custom_call" | custom-call | tf_op jit(solution)/shard_map/attention_forward/pallas_call | solution.py:76
  7.0 0.7 copy-done.3
  7.7 0.7 copy-done.5
  8.3 6.3 %collective-permute-start.2 = (bf16[32,7168]{1,0:T(8,128)(2,1)}, bf16[32,7168]{1,0:T(8,128)(2,1)S(1)}, u32[]{:S(2)}, u32[]{:S(2)}) collective-permute-start(bf16[32,7168]{1,0:T(8,128)(2,1)} %bitcast.55), channel_id=1, source_target_pairs={{0,2},{1,3},{2,0},{3,1},{4,6},{5,7},{6,4},{7,5},{8,10},{9,11},{10,... | collective-permute-start | bytes 1376264 | tf_op jit(solution)/shard_map/ppermute | solution.py:43
  15.3 0.1 stack.86.at_ref
  15.4 0.6 copy-done.7
  16.0 0.9 copy-done.6
  16.9 0.9 copy-done.8
  17.8 4.9 %project.1 = (bf16[32,7168]{1,0:T(8,128)(2,1)S(1)}, bf16[32,7168]{1,0:T(8,128)(2,1)S(1)}, bf16[32,7168]{1,0:T(8,128)(2,1)S(1)}, bf16[32,7168]{1,0:T(8,128)(2,1)S...) custom-call(s32[8]{0:T(128)S(1)} %stack.86.at_ref, ...), custom_call_target="tpu_custom_call" | custom-call | tf_op jit(solution)/shard_map/project/pallas_call | solution.py:106
  22.8 0.4 collective-permute-start.10
  23.3 1.6 %collective-permute-start.4 = (bf16[32,7168]{1,0:T(8,128)(2,1)S(1)}, bf16[32,7168]{1,0:T(8,128)(2,1)S(1)}, u32[]{:S(2)}, u32[]{:S(2)}) collective-permute-start(bf16[32,7168]{1,0:T(8,128)(2,1)S(1)} %get-tuple-element.46), channel_id=1, source_target_pairs={{0,4},{1,13},{2,6},{3,15},{4,8},{5,1},{6,10},{7,3},{8,12},{9,5},{1... | collective-permute-start | bytes 1376264 | tf_op jit(solution)/shard_map/ppermute | solution.py:43
  24.9 7.7 %collective-permute-done.10.rest_3_ = bf16[32,7168]{1,0:T(8,128)(2,1)S(1)} collective-permute-done((bf16[32,7168]{1,0:T(8,128)(2,1)S(1)}, bf16[32,7168]{1,0:T(8,128)(2,1)S(1)}, u32[]{:S(2)}, u32[]{:S(2)}) %collective-permute-start.10) | collective-permute-done | bytes 458784 | tf_op jit(solution)/shard_map/ppermute | solution.py:43
  32.6 1.7 %collective-permute-start.11 = (bf16[32,7168]{1,0:T(8,128)(2,1)S(1)}, bf16[32,7168]{1,0:T(8,128)(2,1)S(1)}, u32[]{:S(2)}, u32[]{:S(2)}) collective-permute-start(bf16[32,7168]{1,0:T(8,128)(2,1)S(1)} %get-tuple-element.55), channel_id=1, source_target_pairs={{0,12},{1,5},{2,14},{3,7},{4,0},{5,9},{6,2},{7,11},{8,4},{9,13},{1... | collective-permute-start | bytes 1376264 | tf_op jit(solution)/shard_map/ppermute | solution.py:43
  34.3 1.2 %collective-permute-start.24 = (bf16[8,7168]{1,0:T(8,128)(2,1)S(1)}, bf16[8,7168]{1,0:T(8,128)(2,1)S(1)}, u32[]{:S(2)}, u32[]{:S(2)}) collective-permute-start(bf16[8,7168]{1,0:T(8,128)(2,1)S(1)} %dynamic-slice_bitcast_fusion), channel_id=1, source_target_pairs={{0,16},{16,0},{32,48},{48,32},{64,80},{80,64},{96,112},{112,96},{1... | collective-permute-start | bytes 344072 | tf_op jit(solution)/shard_map/ppermute | solution.py:43
  35.5 4.3 %collective-permute-done.4 = bf16[32,7168]{1,0:T(8,128)(2,1)S(1)} collective-permute-done((bf16[32,7168]{1,0:T(8,128)(2,1)S(1)}, bf16[32,7168]{1,0:T(8,128)(2,1)S(1)}, u32[]{:S(2)}, u32[]{:S(2)}) %collective-permute-start.4) | collective-permute-done | bytes 458784 | tf_op jit(solution)/shard_map/ppermute | solution.py:43
  39.8 0.9 add_convert_fusion.3
  40.7 0.7 reduce-precision_convert_fusion.2
  41.3 1.4 %collective-permute-done.11 = bf16[32,7168]{1,0:T(8,128)(2,1)S(1)} collective-permute-done((bf16[32,7168]{1,0:T(8,128)(2,1)S(1)}, bf16[32,7168]{1,0:T(8,128)(2,1)S(1)}, u32[]{:S(2)}, u32[]{:S(2)}) %collective-permute-start.11) | collective-permute-done | bytes 458784 | tf_op jit(solution)/shard_map/ppermute | solution.py:43
  42.7 0.5 collective-permute-start.25
  43.3 0.2 copy-done.12
  43.5 0.1 stack.103.at_ref
  43.7 0.6 collective-permute-start.17
  44.3 6.9 %collective-permute-done.5 = bf16[32,7168]{1,0:T(8,128)(2,1)} collective-permute-done((bf16[32,7168]{1,0:T(8,128)(2,1)}, bf16[32,7168]{1,0:T(8,128)(2,1)}, u32[]{:S(2)}, u32[]{:S(2)}) %collective-permute-start.5) | collective-permute-done | bytes 458784 | tf_op jit(solution)/shard_map/ppermute | solution.py:43
  51.1 1.0 reduce-precision_convert_fusion.1
  52.1 1.5 %collective-permute-start.26 = (bf16[8,7168]{1,0:T(8,128)(2,1)S(1)}, bf16[8,7168]{1,0:T(8,128)(2,1)S(1)}, u32[]{:S(2)}, u32[]{:S(2)}) collective-permute-start(bf16[8,7168]{1,0:T(8,128)(2,1)S(1)} %reduce-precision_convert_fusion.1), channel_id=1, source_target_pairs={{0,64},{16,80},{32,96},{48,112},{64,0},{80,16},{96,32},{112,48},{1... | collective-permute-start | bytes 344072 | tf_op jit(solution)/shard_map/ppermute | solution.py:43
  53.6 1.3 %add_convert_fusion.1 = bf16[32,7168]{1,0:T(8,128)(2,1)S(1)} fusion(bf16[32,7168]{1,0:T(8,128)(2,1)} %copy-done.12, bf16[32,7168]{1,0:T(8,128)(2,1)} %collective-permute-done.5, bf16[32,7168]{1,0:T(8,128)(2,1)S(1)} %get-tuple-element.59), kind=kLoop, calls=%fused_computation.1 | loop fusion | flops 1376256 | bytes 1835008 | tf_op jit(solution)/shard_map/convert_element_type | solution.py:214
  55.0 5.4 %collective-permute-done.12.rest_5_ = bf16[32,7168]{1,0:T(8,128)(2,1)S(1)} collective-permute-done((bf16[32,7168]{1,0:T(8,128)(2,1)S(1)}, bf16[32,7168]{1,0:T(8,128)(2,1)S(1)}, u32[]{:S(2)}, u32[]{:S(2)}) %collective-permute-start.12) | collective-permute-done | bytes 458784 | tf_op jit(solution)/shard_map/ppermute | solution.py:43
  60.4 0.1 collective-permute-start.7
  60.6 0.6 collective-permute-start.20
  61.1 0.1 collective-permute-start.19
  61.2 8.8 %collective-permute-done.13.rest_7_ = bf16[32,7168]{1,0:T(8,128)(2,1)S(1)} collective-permute-done((bf16[32,7168]{1,0:T(8,128)(2,1)S(1)}, bf16[32,7168]{1,0:T(8,128)(2,1)S(1)}, u32[]{:S(2)}, u32[]{:S(2)}) %collective-permute-start.13) | collective-permute-done | bytes 458784 | tf_op jit(solution)/shard_map/ppermute | solution.py:43
  70.1 1.5 %collective-permute-start.27 = (bf16[8,7168]{1,0:T(8,128)(2,1)S(1)}, bf16[8,7168]{1,0:T(8,128)(2,1)S(1)}, u32[]{:S(2)}, u32[]{:S(2)}) collective-permute-start(bf16[8,7168]{1,0:T(8,128)(2,1)S(1)} %reduce-precision_convert_fusion), channel_id=1, source_target_pairs={{0,128},{16,144},{32,160},{48,176},{64,192},{80,208},{96,224},{112... | collective-permute-start | bytes 344072 | tf_op jit(solution)/shard_map/ppermute | solution.py:43
  71.6 3.4 %collective-permute-done.7 = bf16[32,7168]{1,0:T(8,128)(2,1)S(1)} collective-permute-done((bf16[32,7168]{1,0:T(8,128)(2,1)}, bf16[32,7168]{1,0:T(8,128)(2,1)S(1)}, u32[]{:S(2)}, u32[]{:S(2)}) %collective-permute-start.7) | collective-permute-done | bytes 458784 | tf_op jit(solution)/shard_map/ppermute | solution.py:43
  75.0 1.1 %add_convert_fusion.2 = bf16[32,7168]{1,0:T(8,128)(2,1)S(1)} fusion(bf16[32,7168]{1,0:T(8,128)(2,1)S(1)} %collective-permute-done.7, bf16[32,7168]{1,0:T(8,128)(2,1)} %copy-done.2), kind=kLoop, calls=%fused_computation.2 | loop fusion | flops 917504 | bytes 1376256 | tf_op jit(solution)/shard_map/convert_element_type | solution.py:214
  76.1 0.1 collective-permute-start.15
  76.3 0.6 collective-permute-start.22
  76.9 2.0 %collective-permute-start.8 = (bf16[32,7168]{1,0:T(8,128)(2,1)S(1)}, bf16[32,7168]{1,0:T(8,128)(2,1)S(1)}, u32[]{:S(2)}, u32[]{:S(2)}) collective-permute-start(bf16[32,7168]{1,0:T(8,128)(2,1)S(1)} %add_convert_fusion.2), channel_id=1, source_target_pairs={{0,4},{1,13},{2,6},{3,15},{4,8},{5,1},{6,10},{7,3},{8,12},{9,5},{1... | collective-permute-start | bytes 1376264 | tf_op jit(solution)/shard_map/ppermute | solution.py:43
  78.9 0.8 collective-permute-start.23
  79.7 0.8 bitcast_subtract_fusion
  80.5 0.6 collective-permute-done.23.rest_15_
  81.1 8.0 %weight_and_context_grads.1 = (bf16[256,7168]{1,0:T(8,128)(2,1)}, bf16[512,256]{1,0:T(8,128)(2,1)S(1)}) custom-call(s32[16]{0:T(128)S(1)} %stack.103.at_ref, bf16[512,256]{1,0:T(8,128)(2,1)S(1)} %copy-done.4, bf16[256,7168]{1,0:T(8,128)(2,1)} %bitcast.60, bf16[32,7168]{1,0:T(8,128)(2,1)S(1)} %bitcast.57, ...), custom_call_target="tpu_custom_call" | custom-call | tf_op jit(solution)/shard_map/weight_and_context_grads/pallas_call | solution.py:153
  89.0 4.6 %attention_backward.1 = (bf16[512,256]{1,0:T(8,128)(2,1)}, bf16[512,256]{1,0:T(8,128)(2,1)}, bf16[512,256]{1,0:T(8,128)(2,1)}) custom-call(bf16[512,256]{1,0:T(8,128)(2,1)} %bitcast.62, bf16[512,256]{1,0:T(8,128)(2,1)} %bitcast.64, bf16[512,256]{1,0:T(8,128)(2,1)} %bitcast.66, bf16[512,256]{1,0:T(8,128)(2,1)S(1)} %get-tuple-element.63.cg_ref), custom_call_target="tpu_custom_call" | custom-call | tf_op jit(solution)/shard_map/attention_backward/pallas_call | solution.py:199
  93.6 9.3 %collective-permute-done.15 = bf16[32,7168]{1,0:T(8,128)(2,1)S(1)} collective-permute-done((bf16[32,7168]{1,0:T(8,128)(2,1)S(1)}, bf16[32,7168]{1,0:T(8,128)(2,1)S(1)}, u32[]{:S(2)}, u32[]{:S(2)}) %collective-permute-start.15) | collective-permute-done | bytes 458784 | tf_op jit(solution)/shard_map/ppermute | solution.py:43
  102.9 1.0 fusion
  (53 shorter events, 0.2 us)
Async XLA Ops:
  0.6 24.2 %copy-start = (bf16[1,2,8,7168]{3,2,1,0:T(8,128)(2,1)S(1)}, bf16[1,2,8,7168]{3,2,1,0:T(8,128)(2,1)}, u32[]{:S(2)}) copy-start(bf16[1,2,8,7168]{3,2,1,0:T(8,128)(2,1)} %param.14) | copy-start | bytes 688132
  0.6 15.4 %collective-permute-start.1 = (bf16[256,7168]{1,0:T(8,128)(2,1)}, bf16[256,7168]{1,0:T(8,128)(2,1)}, u32[]{:S(2)}, u32[]{:S(2)}) collective-permute-start(bf16[256,7168]{1,0:T(8,128)(2,1)} %bitcast.58), channel_id=1, source_target_pairs={{0,1},{1,0},{2,3},{3,2},{4,5},{5,4},{6,7},{7,6},{8,9},{9,8},{10,11... | collective-permute-start | bytes 11010056 | tf_op jit(solution)/shard_map/ppermute | solution.py:43
  0.8 22.1 %collective-permute-start.9 = (bf16[32,7168]{1,0:T(8,128)(2,1)}, bf16[32,7168]{1,0:T(8,128)(2,1)S(1)}, u32[]{:S(2)}, u32[]{:S(2)}) collective-permute-start(bf16[32,7168]{1,0:T(8,128)(2,1)} %bitcast.53), channel_id=1, source_target_pairs={{0,4},{1,13},{2,6},{3,15},{4,8},{5,1},{6,10},{7,3},{8,12},{9,5},{1... | collective-permute-start | bytes 1376264 | tf_op jit(solution)/shard_map/ppermute | solution.py:43
  2.4 20.9 %collective-permute-start.3 = (bf16[32,7168]{1,0:T(8,128)(2,1)}, bf16[32,7168]{1,0:T(8,128)(2,1)S(1)}, u32[]{:S(2)}, u32[]{:S(2)}) collective-permute-start(bf16[32,7168]{1,0:T(8,128)(2,1)} %bitcast.54), channel_id=1, source_target_pairs={{0,12},{1,5},{2,14},{3,7},{4,0},{5,9},{6,2},{7,11},{8,4},{9,13},{1... | collective-permute-start | bytes 1376264 | tf_op jit(solution)/shard_map/ppermute | solution.py:43
  7.0 0.7 copy-start.3
  7.7 0.7 copy-start.5
  8.3 7.0 %collective-permute-start = (bf16[256,256]{1,0:T(8,128)(2,1)S(1)}, bf16[256,256]{1,0:T(8,128)(2,1)S(1)}, u32[]{:S(2)}, u32[]{:S(2)}) collective-permute-start(bf16[256,256]{1,0:T(8,128)(2,1)S(1)} %get-tuple-element.40), channel_id=1, source_target_pairs={{0,1},{1,0},{2,3},{3,2},{4,5},{5,4},{6,7},{7,6},{8,9},{9,8},{10,11... | collective-permute-start | bytes 393224 | tf_op jit(solution)/shard_map/ppermute | solution.py:43
  8.3 35.9 %collective-permute-start.2 = (bf16[32,7168]{1,0:T(8,128)(2,1)}, bf16[32,7168]{1,0:T(8,128)(2,1)S(1)}, u32[]{:S(2)}, u32[]{:S(2)}) collective-permute-start(bf16[32,7168]{1,0:T(8,128)(2,1)} %bitcast.55), channel_id=1, source_target_pairs={{0,2},{1,3},{2,0},{3,1},{4,6},{5,7},{6,4},{7,5},{8,10},{9,11},{10,... | collective-permute-start | bytes 1376264 | tf_op jit(solution)/shard_map/ppermute | solution.py:43
  15.4 0.7 copy-start.7
  16.0 0.9 copy-start.6
  16.9 0.9 copy-start.8
  17.8 25.7 %copy-start.1 = (bf16[1,32,7168]{2,1,0:T(8,128)(2,1)S(1)}, bf16[1,32,7168]{2,1,0:T(8,128)(2,1)}, u32[]{:S(2)}) copy-start(bf16[1,32,7168]{2,1,0:T(8,128)(2,1)} %param.13) | copy-start | bytes 1376260
  22.8 19.9 %copy-start.2 = (bf16[32,7168]{1,0:T(8,128)(2,1)}, bf16[32,7168]{1,0:T(8,128)(2,1)S(1)}, u32[]{:S(2)}) copy-start(bf16[32,7168]{1,0:T(8,128)(2,1)S(1)} %get-tuple-element.42) | copy-start | bytes 1376260
  22.8 20.4 %copy-start.9 = (bf16[32,7168]{1,0:T(8,128)(2,1)}, bf16[32,7168]{1,0:T(8,128)(2,1)S(1)}, u32[]{:S(2)}) copy-start(bf16[32,7168]{1,0:T(8,128)(2,1)S(1)} %get-tuple-element.58) | copy-start | bytes 1376260
  22.8 20.4 %copy-start.11 = (bf16[32,7168]{1,0:T(8,128)(2,1)}, bf16[32,7168]{1,0:T(8,128)(2,1)S(1)}, u32[]{:S(2)}) copy-start(bf16[32,7168]{1,0:T(8,128)(2,1)S(1)} %get-tuple-element.49) | copy-start | bytes 1376260
  22.8 9.8 %collective-permute-start.10 = (bf16[32,7168]{1,0:T(8,128)(2,1)S(1)}, bf16[32,7168]{1,0:T(8,128)(2,1)S(1)}, u32[]{:S(2)}, u32[]{:S(2)}) collective-permute-start(bf16[32,7168]{1,0:T(8,128)(2,1)S(1)} %collective-permute-done.9.rest_1_), channel_id=1, source_target_pairs={{0,4},{1,13},{2,6},{3,15},{4,8},{5,1},{6,10},{7,3},{8,12},{9,5},{1... | collective-permute-start | bytes 1376264 | tf_op jit(solution)/shard_map/ppermute | solution.py:43
  23.3 16.5 %collective-permute-start.4 = (bf16[32,7168]{1,0:T(8,128)(2,1)S(1)}, bf16[32,7168]{1,0:T(8,128)(2,1)S(1)}, u32[]{:S(2)}, u32[]{:S(2)}) collective-permute-start(bf16[32,7168]{1,0:T(8,128)(2,1)S(1)} %get-tuple-element.46), channel_id=1, source_target_pairs={{0,4},{1,13},{2,6},{3,15},{4,8},{5,1},{6,10},{7,3},{8,12},{9,5},{1... | collective-permute-start | bytes 1376264 | tf_op jit(solution)/shard_map/ppermute | solution.py:43
  32.6 10.1 %collective-permute-start.11 = (bf16[32,7168]{1,0:T(8,128)(2,1)S(1)}, bf16[32,7168]{1,0:T(8,128)(2,1)S(1)}, u32[]{:S(2)}, u32[]{:S(2)}) collective-permute-start(bf16[32,7168]{1,0:T(8,128)(2,1)S(1)} %get-tuple-element.55), channel_id=1, source_target_pairs={{0,12},{1,5},{2,14},{3,7},{4,0},{5,9},{6,2},{7,11},{8,4},{9,13},{1... | collective-permute-start | bytes 1376264 | tf_op jit(solution)/shard_map/ppermute | solution.py:43
  34.3 6.4 %collective-permute-start.24 = (bf16[8,7168]{1,0:T(8,128)(2,1)S(1)}, bf16[8,7168]{1,0:T(8,128)(2,1)S(1)}, u32[]{:S(2)}, u32[]{:S(2)}) collective-permute-start(bf16[8,7168]{1,0:T(8,128)(2,1)S(1)} %dynamic-slice_bitcast_fusion), channel_id=1, source_target_pairs={{0,16},{16,0},{32,48},{48,32},{64,80},{80,64},{96,112},{112,96},{1... | collective-permute-start | bytes 344072 | tf_op jit(solution)/shard_map/ppermute | solution.py:43
  40.7 10.5 %collective-permute-start.5 = (bf16[32,7168]{1,0:T(8,128)(2,1)}, bf16[32,7168]{1,0:T(8,128)(2,1)}, u32[]{:S(2)}, u32[]{:S(2)}) collective-permute-start(bf16[32,7168]{1,0:T(8,128)(2,1)} %add_convert_fusion.3), channel_id=1, source_target_pairs={{0,4},{1,13},{2,6},{3,15},{4,8},{5,1},{6,10},{7,3},{8,12},{9,5},{1... | collective-permute-start | bytes 1376264 | tf_op jit(solution)/shard_map/ppermute | solution.py:43
  42.7 0.8 copy-start.12
  42.7 8.4 %collective-permute-start.25 = (bf16[8,7168]{1,0:T(8,128)(2,1)}, bf16[8,7168]{1,0:T(8,128)(2,1)}, u32[]{:S(2)}, u32[]{:S(2)}) collective-permute-start(bf16[8,7168]{1,0:T(8,128)(2,1)} %reduce-precision_convert_fusion.2), channel_id=1, source_target_pairs={{0,32},{16,48},{32,0},{48,16},{64,96},{80,112},{96,64},{112,80},{1... | collective-permute-start | bytes 344072 | tf_op jit(solution)/shard_map/ppermute | solution.py:43
  43.5 17.0 %collective-permute-start.16 = (bf16[32,7168]{1,0:T(8,128)(2,1)S(1)}, bf16[32,7168]{1,0:T(8,128)(2,1)}, u32[]{:S(2)}, u32[]{:S(2)}) collective-permute-start(bf16[32,7168]{1,0:T(8,128)(2,1)S(1)} %bitcast.56), channel_id=1, source_target_pairs={{0,1},{1,0},{2,3},{3,2},{4,5},{5,4},{6,7},{7,6},{8,9},{9,8},{10,11... | collective-permute-start | bytes 1376264 | tf_op jit(solution)/shard_map/ppermute | solution.py:43
  43.6 33.2 %copy-start.10 = (bf16[32,7168]{1,0:T(8,128)(2,1)S(1)}, bf16[32,7168]{1,0:T(8,128)(2,1)}, u32[]{:S(2)}) copy-start(bf16[32,7168]{1,0:T(8,128)(2,1)} %copy-done.9) | copy-start | bytes 1376260
  43.6 36.0 %copy-start.13 = (f32[2,8,7168]{2,1,0:T(8,128)S(1)}, f32[2,8,7168]{2,1,0:T(8,128)}, u32[]{:S(2)}) copy-start(f32[2,8,7168]{2,1,0:T(8,128)} %param.15) | copy-start | bytes 1376260
  43.6 36.0 %copy-start.14 = (f32[2,8,7168]{2,1,0:T(8,128)S(1)}, f32[2,8,7168]{2,1,0:T(8,128)}, u32[]{:S(2)}) copy-start(f32[2,8,7168]{2,1,0:T(8,128)} %param.16) | copy-start | bytes 1376260
  43.6 37.4 %copy-start.4 = (bf16[512,256]{1,0:T(8,128)(2,1)S(1)}, bf16[512,256]{1,0:T(8,128)(2,1)}, u32[]{:S(2)}) copy-start(bf16[512,256]{1,0:T(8,128)(2,1)} %copy-done.3) | copy-start | bytes 786436
  43.7 17.5 %collective-permute-start.17 = (bf16[32,7168]{1,0:T(8,128)(2,1)S(1)}, bf16[32,7168]{1,0:T(8,128)(2,1)S(1)}, u32[]{:S(2)}, u32[]{:S(2)}) collective-permute-start(bf16[32,7168]{1,0:T(8,128)(2,1)S(1)} %collective-permute-done.9.rest_1_), channel_id=1, source_target_pairs={{0,1},{1,0},{2,3},{3,2},{4,5},{5,4},{6,7},{7,6},{8,9},{9,8},{10,11... | collective-permute-start | bytes 1376264 | tf_op jit(solution)/shard_map/ppermute | solution.py:43
  44.3 16.1 %collective-permute-start.12 = (bf16[32,7168]{1,0:T(8,128)(2,1)S(1)}, bf16[32,7168]{1,0:T(8,128)(2,1)S(1)}, u32[]{:S(2)}, u32[]{:S(2)}) collective-permute-start(bf16[32,7168]{1,0:T(8,128)(2,1)S(1)} %collective-permute-done.2.rest_4_), channel_id=1, source_target_pairs={{0,4},{1,13},{2,6},{3,15},{4,8},{5,1},{6,10},{7,3},{8,12},{9,5},{1... | collective-permute-start | bytes 1376264 | tf_op jit(solution)/shard_map/ppermute | solution.py:43
  51.1 9.3 %collective-permute-start.6 = (bf16[32,7168]{1,0:T(8,128)(2,1)S(1)}, bf16[32,7168]{1,0:T(8,128)(2,1)S(1)}, u32[]{:S(2)}, u32[]{:S(2)}) collective-permute-start(bf16[32,7168]{1,0:T(8,128)(2,1)S(1)} %collective-permute-done.2.rest_4_), channel_id=1, source_target_pairs={{0,12},{1,5},{2,14},{3,7},{4,0},{5,9},{6,2},{7,11},{8,4},{9,13},{1... | collective-permute-start | bytes 1376264 | tf_op jit(solution)/shard_map/ppermute | solution.py:43
  52.1 8.3 %collective-permute-start.26 = (bf16[8,7168]{1,0:T(8,128)(2,1)S(1)}, bf16[8,7168]{1,0:T(8,128)(2,1)S(1)}, u32[]{:S(2)}, u32[]{:S(2)}) collective-permute-start(bf16[8,7168]{1,0:T(8,128)(2,1)S(1)} %reduce-precision_convert_fusion.1), channel_id=1, source_target_pairs={{0,64},{16,80},{32,96},{48,112},{64,0},{80,16},{96,32},{112,48},{1... | collective-permute-start | bytes 344072 | tf_op jit(solution)/shard_map/ppermute | solution.py:43
  60.4 15.7 %collective-permute-start.18 = (bf16[32,7168]{1,0:T(8,128)(2,1)S(1)}, bf16[32,7168]{1,0:T(8,128)(2,1)S(1)}, u32[]{:S(2)}, u32[]{:S(2)}) collective-permute-start(bf16[32,7168]{1,0:T(8,128)(2,1)S(1)} %collective-permute-done.3.rest_2_), channel_id=1, source_target_pairs={{0,1},{1,0},{2,3},{3,2},{4,5},{5,4},{6,7},{7,6},{8,9},{9,8},{10,11... | collective-permute-start | bytes 1376264 | tf_op jit(solution)/shard_map/ppermute | solution.py:43
  60.4 9.7 %collective-permute-start.13 = (bf16[32,7168]{1,0:T(8,128)(2,1)S(1)}, bf16[32,7168]{1,0:T(8,128)(2,1)S(1)}, u32[]{:S(2)}, u32[]{:S(2)}) collective-permute-start(bf16[32,7168]{1,0:T(8,128)(2,1)S(1)} %collective-permute-done.12.rest_5_), channel_id=1, source_target_pairs={{0,4},{1,13},{2,6},{3,15},{4,8},{5,1},{6,10},{7,3},{8,12},{9,5},{1... | collective-permute-start | bytes 1376264 | tf_op jit(solution)/shard_map/ppermute | solution.py:43
  60.4 14.6 %collective-permute-start.7 = (bf16[32,7168]{1,0:T(8,128)(2,1)}, bf16[32,7168]{1,0:T(8,128)(2,1)S(1)}, u32[]{:S(2)}, u32[]{:S(2)}) collective-permute-start(bf16[32,7168]{1,0:T(8,128)(2,1)} %copy-done.11), channel_id=1, source_target_pairs={{0,4},{1,13},{2,6},{3,15},{4,8},{5,1},{6,10},{7,3},{8,12},{9,5},{1... | collective-permute-start | bytes 1376264 | tf_op jit(solution)/shard_map/ppermute | solution.py:43
  60.6 15.7 %collective-permute-start.20 = (bf16[32,7168]{1,0:T(8,128)(2,1)S(1)}, bf16[32,7168]{1,0:T(8,128)(2,1)S(1)}, u32[]{:S(2)}, u32[]{:S(2)}) collective-permute-start(bf16[32,7168]{1,0:T(8,128)(2,1)S(1)} %collective-permute-done.2.rest_4_), channel_id=1, source_target_pairs={{0,1},{1,0},{2,3},{3,2},{4,5},{5,4},{6,7},{7,6},{8,9},{9,8},{10,11... | collective-permute-start | bytes 1376264 | tf_op jit(solution)/shard_map/ppermute | solution.py:43
  61.1 15.7 %collective-permute-start.19 = (bf16[32,7168]{1,0:T(8,128)(2,1)S(1)}, bf16[32,7168]{1,0:T(8,128)(2,1)S(1)}, u32[]{:S(2)}, u32[]{:S(2)}) collective-permute-start(bf16[32,7168]{1,0:T(8,128)(2,1)S(1)} %collective-permute-done.10.rest_3_), channel_id=1, source_target_pairs={{0,1},{1,0},{2,3},{3,2},{4,5},{5,4},{6,7},{7,6},{8,9},{9,8},{10,11... | collective-permute-start | bytes 1376264 | tf_op jit(solution)/shard_map/ppermute | solution.py:43
  70.1 6.8 %collective-permute-start.27 = (bf16[8,7168]{1,0:T(8,128)(2,1)S(1)}, bf16[8,7168]{1,0:T(8,128)(2,1)S(1)}, u32[]{:S(2)}, u32[]{:S(2)}) collective-permute-start(bf16[8,7168]{1,0:T(8,128)(2,1)S(1)} %reduce-precision_convert_fusion), channel_id=1, source_target_pairs={{0,128},{16,144},{32,160},{48,176},{64,192},{80,208},{96,224},{112... | collective-permute-start | bytes 344072 | tf_op jit(solution)/shard_map/ppermute | solution.py:43
  75.0 3.9 %collective-permute-start.21 = (bf16[32,7168]{1,0:T(8,128)(2,1)S(1)}, bf16[32,7168]{1,0:T(8,128)(2,1)S(1)}, u32[]{:S(2)}, u32[]{:S(2)}) collective-permute-start(bf16[32,7168]{1,0:T(8,128)(2,1)S(1)} %collective-permute-done.12.rest_5_), channel_id=1, source_target_pairs={{0,1},{1,0},{2,3},{3,2},{4,5},{5,4},{6,7},{7,6},{8,9},{9,8},{10,11... | collective-permute-start | bytes 1376264 | tf_op jit(solution)/shard_map/ppermute | solution.py:43
  76.1 26.8 %collective-permute-start.15 = (bf16[32,7168]{1,0:T(8,128)(2,1)S(1)}, bf16[32,7168]{1,0:T(8,128)(2,1)S(1)}, u32[]{:S(2)}, u32[]{:S(2)}) collective-permute-start(bf16[32,7168]{1,0:T(8,128)(2,1)S(1)} %add_convert_fusion.1), channel_id=1, source_target_pairs={{0,2},{1,3},{2,0},{3,1},{4,6},{5,7},{6,4},{7,5},{8,10},{9,11},{10,... | collective-permute-start | bytes 1376264 | tf_op jit(solution)/shard_map/ppermute | solution.py:43
  76.3 4.2 %collective-permute-start.22 = (bf16[32,7168]{1,0:T(8,128)(2,1)S(1)}, bf16[32,7168]{1,0:T(8,128)(2,1)S(1)}, u32[]{:S(2)}, u32[]{:S(2)}) collective-permute-start(bf16[32,7168]{1,0:T(8,128)(2,1)S(1)} %collective-permute-done.6.rest_6_), channel_id=1, source_target_pairs={{0,1},{1,0},{2,3},{3,2},{4,5},{5,4},{6,7},{7,6},{8,9},{9,8},{10,11... | collective-permute-start | bytes 1376264 | tf_op jit(solution)/shard_map/ppermute | solution.py:43
  76.9 26.0 %collective-permute-start.14 = (bf16[32,7168]{1,0:T(8,128)(2,1)S(1)}, bf16[32,7168]{1,0:T(8,128)(2,1)S(1)}, u32[]{:S(2)}, u32[]{:S(2)}) collective-permute-start(bf16[32,7168]{1,0:T(8,128)(2,1)S(1)} %copy-done.10), channel_id=1, source_target_pairs={{0,12},{1,5},{2,14},{3,7},{4,0},{5,9},{6,2},{7,11},{8,4},{9,13},{1... | collective-permute-start | bytes 1376264 | tf_op jit(solution)/shard_map/ppermute | solution.py:43
  76.9 26.0 %collective-permute-start.8 = (bf16[32,7168]{1,0:T(8,128)(2,1)S(1)}, bf16[32,7168]{1,0:T(8,128)(2,1)S(1)}, u32[]{:S(2)}, u32[]{:S(2)}) collective-permute-start(bf16[32,7168]{1,0:T(8,128)(2,1)S(1)} %add_convert_fusion.2), channel_id=1, source_target_pairs={{0,4},{1,13},{2,6},{3,15},{4,8},{5,1},{6,10},{7,3},{8,12},{9,5},{1... | collective-permute-start | bytes 1376264 | tf_op jit(solution)/shard_map/ppermute | solution.py:43
  78.9 2.2 %collective-permute-start.23 = (bf16[32,7168]{1,0:T(8,128)(2,1)S(1)}, bf16[32,7168]{1,0:T(8,128)(2,1)S(1)}, u32[]{:S(2)}, u32[]{:S(2)}) collective-permute-start(bf16[32,7168]{1,0:T(8,128)(2,1)S(1)} %collective-permute-done.13.rest_7_), channel_id=1, source_target_pairs={{0,1},{1,0},{2,3},{3,2},{4,5},{5,4},{6,7},{7,6},{8,9},{9,8},{10,11... | collective-permute-start | bytes 1376264 | tf_op jit(solution)/shard_map/ppermute | solution.py:43

commit v3 on v2

--- a/solution.py
+++ b/solution.py
@@ -293,7 +293,7 @@
     part = lax.dynamic_index_in_dim(local_params[0], chosen, 0, keepdims=False)
     outer_old = lax.dynamic_index_in_dim(global_params, chosen, 0, keepdims=False)
     moment_old = lax.dynamic_index_in_dim(momentum, chosen, 0, keepdims=False)
-    for moves, ready in zip(REP_STEPS, (near3, side, middle, far1)):
+    for moves, ready in zip(REP_STEPS, (near3, side, second, far1)):
         part = after(part, ready)
         total = part.astype(F32) + send(part, moves, "rep").astype(F32)
         part = lax.reduce_precision(total, 8, 7).astype(BF16)

time: 104 us -> 104 us (level)
  no operation moved by 1% of the time
where the time goes in v3:
time: 104 us
  waiting for transfers between devices  47.9 us (46%)
  starting transfers between devices  22.9 us (22%)
  Pallas kernels  20.4 us (20%)
  other arithmetic  6.86 us (7%)
  local copies, waits for them, and re-layouts  4.3 us (4%)
  between operations  1.52 us (1%)
    ppermute x28, waiting for transfers between devices, send(): return lax.ppermute(value, axis, moves)  47.9 us
    ppermute x28, starting transfers between devices, send(): return lax.ppermute(value, axis, moves)  22.9 us
    pallas_call x1, Pallas kernels, weight_and_context_grads(): pl.pallas_call(functools.partial(weight_kernel, n), grid=(width // blk,),...  7.96 us
    pallas_call x1, Pallas kernels, project(): pl.pallas_call(project_kernel, grid=(width // blk,), in_specs=[pl.BlockSp...  4.94 us
    pallas_call x1, Pallas kernels, attention_backward(): pl.pallas_call(backward_kernel, in_specs=[vmem] * 4, out_specs=[vmem] * 3...  4.57 us
    unnamed x30, local copies, waits for them, and re-layouts  4.11 us
    convert_element_type x3, other arithmetic, add(): return total.astype(BF16)  3.32 us
    pallas_call x1, Pallas kernels, attention_forward(): pl.pallas_call(forward_kernel, in_specs=[pl.BlockSpec(memory_space=SMEM),...  2.9 us
  transfers between devices with their start and end apart: 28, of which 9 were waited for; matrix products, arithmetic and copies ran while one was open for 6% of the time, Pallas kernels for 20%

profile of v3, /device:TPU:36, one launch (start us, length us, event | category | flops | bytes accessed | tf_op | source)
XLA Modules:
  0.0 103.9 jit_solution(7340716072055967403)
XLA Ops:
  0.6 0.0 copy-start
  0.6 0.1 collective-permute-start.1
  0.8 1.7 %collective-permute-start.9 = (bf16[32,7168]{1,0:T(8,128)(2,1)}, bf16[32,7168]{1,0:T(8,128)(2,1)S(1)}, u32[]{:S(2)}, u32[]{:S(2)}) collective-permute-start(bf16[32,7168]{1,0:T(8,128)(2,1)} %bitcast.53), channel_id=1, source_target_pairs={{0,4},{1,13},{2,6},{3,15},{4,8},{5,1},{6,10},{7,3},{8,12},{9,5},{1... | collective-permute-start | bytes 1376264 | tf_op jit(solution)/shard_map/ppermute | solution.py:43
  2.4 1.7 %collective-permute-start.3 = (bf16[32,7168]{1,0:T(8,128)(2,1)}, bf16[32,7168]{1,0:T(8,128)(2,1)S(1)}, u32[]{:S(2)}, u32[]{:S(2)}) collective-permute-start(bf16[32,7168]{1,0:T(8,128)(2,1)} %bitcast.54), channel_id=1, source_target_pairs={{0,12},{1,5},{2,14},{3,7},{4,0},{5,9},{6,2},{7,11},{8,4},{9,13},{1... | collective-permute-start | bytes 1376264 | tf_op jit(solution)/shard_map/ppermute | solution.py:43
  4.1 2.9 %attention_forward.1 = (bf16[512,256]{1,0:T(8,128)(2,1)S(1)}, bf16[256,256]{1,0:T(8,128)(2,1)S(1)}, bf16[256,256]{1,0:T(8,128)(2,1)S(1)}) custom-call(s32[1]{0:T(128)} %bitcast.8.core_ref, bf16[512,256]{1,0:T(8,128)(2,1)} %bitcast.61, bf16[512,256]{1,0:T(8,128)(2,1)} %bitcast.63, bf16[512,256]{1,0:T(8,128)(2,1)} %bitcast.65), custom_call_target="tpu_custom_call" | custom-call | tf_op jit(solution)/shard_map/attention_forward/pallas_call | solution.py:76
  7.0 0.7 copy-done.3
  7.7 0.7 copy-done.5
  8.3 6.3 %collective-permute-start.2 = (bf16[32,7168]{1,0:T(8,128)(2,1)}, bf16[32,7168]{1,0:T(8,128)(2,1)S(1)}, u32[]{:S(2)}, u32[]{:S(2)}) collective-permute-start(bf16[32,7168]{1,0:T(8,128)(2,1)} %bitcast.55), channel_id=1, source_target_pairs={{0,2},{1,3},{2,0},{3,1},{4,6},{5,7},{6,4},{7,5},{8,10},{9,11},{10,... | collective-permute-start | bytes 1376264 | tf_op jit(solution)/shard_map/ppermute | solution.py:43
  15.3 0.1 stack.86.at_ref
  15.4 0.6 copy-done.7
  16.0 0.9 copy-done.6
  16.9 0.9 copy-done.8
  17.8 4.9 %project.1 = (bf16[32,7168]{1,0:T(8,128)(2,1)S(1)}, bf16[32,7168]{1,0:T(8,128)(2,1)S(1)}, bf16[32,7168]{1,0:T(8,128)(2,1)S(1)}, bf16[32,7168]{1,0:T(8,128)(2,1)S...) custom-call(s32[8]{0:T(128)S(1)} %stack.86.at_ref, ...), custom_call_target="tpu_custom_call" | custom-call | tf_op jit(solution)/shard_map/project/pallas_call | solution.py:106
  22.8 0.4 collective-permute-start.10
  23.3 1.6 %collective-permute-start.4 = (bf16[32,7168]{1,0:T(8,128)(2,1)S(1)}, bf16[32,7168]{1,0:T(8,128)(2,1)S(1)}, u32[]{:S(2)}, u32[]{:S(2)}) collective-permute-start(bf16[32,7168]{1,0:T(8,128)(2,1)S(1)} %get-tuple-element.46), channel_id=1, source_target_pairs={{0,4},{1,13},{2,6},{3,15},{4,8},{5,1},{6,10},{7,3},{8,12},{9,5},{1... | collective-permute-start | bytes 1376264 | tf_op jit(solution)/shard_map/ppermute | solution.py:43
  24.9 7.7 %collective-permute-done.10.rest_3_ = bf16[32,7168]{1,0:T(8,128)(2,1)S(1)} collective-permute-done((bf16[32,7168]{1,0:T(8,128)(2,1)S(1)}, bf16[32,7168]{1,0:T(8,128)(2,1)S(1)}, u32[]{:S(2)}, u32[]{:S(2)}) %collective-permute-start.10) | collective-permute-done | bytes 458784 | tf_op jit(solution)/shard_map/ppermute | solution.py:43
  32.6 1.7 %collective-permute-start.11 = (bf16[32,7168]{1,0:T(8,128)(2,1)S(1)}, bf16[32,7168]{1,0:T(8,128)(2,1)S(1)}, u32[]{:S(2)}, u32[]{:S(2)}) collective-permute-start(bf16[32,7168]{1,0:T(8,128)(2,1)S(1)} %get-tuple-element.55), channel_id=1, source_target_pairs={{0,12},{1,5},{2,14},{3,7},{4,0},{5,9},{6,2},{7,11},{8,4},{9,13},{1... | collective-permute-start | bytes 1376264 | tf_op jit(solution)/shard_map/ppermute | solution.py:43
  34.3 1.2 %collective-permute-start.24 = (bf16[8,7168]{1,0:T(8,128)(2,1)S(1)}, bf16[8,7168]{1,0:T(8,128)(2,1)S(1)}, u32[]{:S(2)}, u32[]{:S(2)}) collective-permute-start(bf16[8,7168]{1,0:T(8,128)(2,1)S(1)} %dynamic-slice_bitcast_fusion), channel_id=1, source_target_pairs={{0,16},{16,0},{32,48},{48,32},{64,80},{80,64},{96,112},{112,96},{1... | collective-permute-start | bytes 344072 | tf_op jit(solution)/shard_map/ppermute | solution.py:43
  35.5 4.3 %collective-permute-done.4 = bf16[32,7168]{1,0:T(8,128)(2,1)S(1)} collective-permute-done((bf16[32,7168]{1,0:T(8,128)(2,1)S(1)}, bf16[32,7168]{1,0:T(8,128)(2,1)S(1)}, u32[]{:S(2)}, u32[]{:S(2)}) %collective-permute-start.4) | collective-permute-done | bytes 458784 | tf_op jit(solution)/shard_map/ppermute | solution.py:43
  39.8 0.9 add_convert_fusion.3
  40.7 0.7 reduce-precision_convert_fusion.2
  41.3 1.4 %collective-permute-done.11 = bf16[32,7168]{1,0:T(8,128)(2,1)S(1)} collective-permute-done((bf16[32,7168]{1,0:T(8,128)(2,1)S(1)}, bf16[32,7168]{1,0:T(8,128)(2,1)S(1)}, u32[]{:S(2)}, u32[]{:S(2)}) %collective-permute-start.11) | collective-permute-done | bytes 458784 | tf_op jit(solution)/shard_map/ppermute | solution.py:43
  42.7 0.5 collective-permute-start.25
  43.3 0.2 copy-done.12
  43.5 0.1 stack.103.at_ref
  43.7 0.6 collective-permute-start.17
  44.3 6.9 %collective-permute-done.5 = bf16[32,7168]{1,0:T(8,128)(2,1)} collective-permute-done((bf16[32,7168]{1,0:T(8,128)(2,1)}, bf16[32,7168]{1,0:T(8,128)(2,1)}, u32[]{:S(2)}, u32[]{:S(2)}) %collective-permute-start.5) | collective-permute-done | bytes 458784 | tf_op jit(solution)/shard_map/ppermute | solution.py:43
  51.1 1.0 reduce-precision_convert_fusion.1
  52.1 1.5 %collective-permute-start.26 = (bf16[8,7168]{1,0:T(8,128)(2,1)S(1)}, bf16[8,7168]{1,0:T(8,128)(2,1)S(1)}, u32[]{:S(2)}, u32[]{:S(2)}) collective-permute-start(bf16[8,7168]{1,0:T(8,128)(2,1)S(1)} %reduce-precision_convert_fusion.1), channel_id=1, source_target_pairs={{0,64},{16,80},{32,96},{48,112},{64,0},{80,16},{96,32},{112,48},{1... | collective-permute-start | bytes 344072 | tf_op jit(solution)/shard_map/ppermute | solution.py:43
  53.6 1.3 %add_convert_fusion.1 = bf16[32,7168]{1,0:T(8,128)(2,1)S(1)} fusion(bf16[32,7168]{1,0:T(8,128)(2,1)} %copy-done.12, bf16[32,7168]{1,0:T(8,128)(2,1)} %collective-permute-done.5, bf16[32,7168]{1,0:T(8,128)(2,1)S(1)} %get-tuple-element.59), kind=kLoop, calls=%fused_computation.1 | loop fusion | flops 1376256 | bytes 1835008 | tf_op jit(solution)/shard_map/convert_element_type | solution.py:214
  55.0 5.4 %collective-permute-done.12.rest_5_ = bf16[32,7168]{1,0:T(8,128)(2,1)S(1)} collective-permute-done((bf16[32,7168]{1,0:T(8,128)(2,1)S(1)}, bf16[32,7168]{1,0:T(8,128)(2,1)S(1)}, u32[]{:S(2)}, u32[]{:S(2)}) %collective-permute-start.12) | collective-permute-done | bytes 458784 | tf_op jit(solution)/shard_map/ppermute | solution.py:43
  60.4 0.1 collective-permute-start.7
  60.6 0.6 collective-permute-start.20
  61.1 0.1 collective-permute-start.19
  61.2 8.8 %collective-permute-done.13.rest_7_ = bf16[32,7168]{1,0:T(8,128)(2,1)S(1)} collective-permute-done((bf16[32,7168]{1,0:T(8,128)(2,1)S(1)}, bf16[32,7168]{1,0:T(8,128)(2,1)S(1)}, u32[]{:S(2)}, u32[]{:S(2)}) %collective-permute-start.13) | collective-permute-done | bytes 458784 | tf_op jit(solution)/shard_map/ppermute | solution.py:43
  70.1 1.5 %collective-permute-start.27 = (bf16[8,7168]{1,0:T(8,128)(2,1)S(1)}, bf16[8,7168]{1,0:T(8,128)(2,1)S(1)}, u32[]{:S(2)}, u32[]{:S(2)}) collective-permute-start(bf16[8,7168]{1,0:T(8,128)(2,1)S(1)} %reduce-precision_convert_fusion), channel_id=1, source_target_pairs={{0,128},{16,144},{32,160},{48,176},{64,192},{80,208},{96,224},{112... | collective-permute-start | bytes 344072 | tf_op jit(solution)/shard_map/ppermute | solution.py:43
  71.6 3.4 %collective-permute-done.7 = bf16[32,7168]{1,0:T(8,128)(2,1)S(1)} collective-permute-done((bf16[32,7168]{1,0:T(8,128)(2,1)}, bf16[32,7168]{1,0:T(8,128)(2,1)S(1)}, u32[]{:S(2)}, u32[]{:S(2)}) %collective-permute-start.7) | collective-permute-done | bytes 458784 | tf_op jit(solution)/shard_map/ppermute | solution.py:43
  75.0 1.1 %add_convert_fusion.2 = bf16[32,7168]{1,0:T(8,128)(2,1)S(1)} fusion(bf16[32,7168]{1,0:T(8,128)(2,1)S(1)} %collective-permute-done.7, bf16[32,7168]{1,0:T(8,128)(2,1)} %copy-done.2), kind=kLoop, calls=%fused_computation.2 | loop fusion | flops 917504 | bytes 1376256 | tf_op jit(solution)/shard_map/convert_element_type | solution.py:214
  76.1 0.1 collective-permute-start.15
  76.3 0.6 collective-permute-start.22
  76.9 2.0 %collective-permute-start.8 = (bf16[32,7168]{1,0:T(8,128)(2,1)S(1)}, bf16[32,7168]{1,0:T(8,128)(2,1)S(1)}, u32[]{:S(2)}, u32[]{:S(2)}) collective-permute-start(bf16[32,7168]{1,0:T(8,128)(2,1)S(1)} %add_convert_fusion.2), channel_id=1, source_target_pairs={{0,4},{1,13},{2,6},{3,15},{4,8},{5,1},{6,10},{7,3},{8,12},{9,5},{1... | collective-permute-start | bytes 1376264 | tf_op jit(solution)/shard_map/ppermute | solution.py:43
  78.9 0.8 collective-permute-start.23
  79.7 0.8 bitcast_subtract_fusion
  80.5 0.6 collective-permute-done.23.rest_15_
  81.1 8.0 %weight_and_context_grads.1 = (bf16[256,7168]{1,0:T(8,128)(2,1)}, bf16[512,256]{1,0:T(8,128)(2,1)S(1)}) custom-call(s32[16]{0:T(128)S(1)} %stack.103.at_ref, bf16[512,256]{1,0:T(8,128)(2,1)S(1)} %copy-done.4, bf16[256,7168]{1,0:T(8,128)(2,1)} %bitcast.60, bf16[32,7168]{1,0:T(8,128)(2,1)S(1)} %bitcast.57, ...), custom_call_target="tpu_custom_call" | custom-call | tf_op jit(solution)/shard_map/weight_and_context_grads/pallas_call | solution.py:153
  89.0 4.6 %attention_backward.1 = (bf16[512,256]{1,0:T(8,128)(2,1)}, bf16[512,256]{1,0:T(8,128)(2,1)}, bf16[512,256]{1,0:T(8,128)(2,1)}) custom-call(bf16[512,256]{1,0:T(8,128)(2,1)} %bitcast.62, bf16[512,256]{1,0:T(8,128)(2,1)} %bitcast.64, bf16[512,256]{1,0:T(8,128)(2,1)} %bitcast.66, bf16[512,256]{1,0:T(8,128)(2,1)S(1)} %get-tuple-element.63.cg_ref), custom_call_target="tpu_custom_call" | custom-call | tf_op jit(solution)/shard_map/attention_backward/pallas_call | solution.py:199
  93.6 9.3 %collective-permute-done.15 = bf16[32,7168]{1,0:T(8,128)(2,1)S(1)} collective-permute-done((bf16[32,7168]{1,0:T(8,128)(2,1)S(1)}, bf16[32,7168]{1,0:T(8,128)(2,1)S(1)}, u32[]{:S(2)}, u32[]{:S(2)}) %collective-permute-start.15) | collective-permute-done | bytes 458784 | tf_op jit(solution)/shard_map/ppermute | solution.py:43
  102.9 1.0 fusion
  (53 shorter events, 0.2 us)
Async XLA Ops:
  0.6 24.2 %copy-start = (bf16[1,2,8,7168]{3,2,1,0:T(8,128)(2,1)S(1)}, bf16[1,2,8,7168]{3,2,1,0:T(8,128)(2,1)}, u32[]{:S(2)}) copy-start(bf16[1,2,8,7168]{3,2,1,0:T(8,128)(2,1)} %param.14) | copy-start | bytes 688132
  0.6 15.4 %collective-permute-start.1 = (bf16[256,7168]{1,0:T(8,128)(2,1)}, bf16[256,7168]{1,0:T(8,128)(2,1)}, u32[]{:S(2)}, u32[]{:S(2)}) collective-permute-start(bf16[256,7168]{1,0:T(8,128)(2,1)} %bitcast.58), channel_id=1, source_target_pairs={{0,1},{1,0},{2,3},{3,2},{4,5},{5,4},{6,7},{7,6},{8,9},{9,8},{10,11... | collective-permute-start | bytes 11010056 | tf_op jit(solution)/shard_map/ppermute | solution.py:43
  0.8 22.1 %collective-permute-start.9 = (bf16[32,7168]{1,0:T(8,128)(2,1)}, bf16[32,7168]{1,0:T(8,128)(2,1)S(1)}, u32[]{:S(2)}, u32[]{:S(2)}) collective-permute-start(bf16[32,7168]{1,0:T(8,128)(2,1)} %bitcast.53), channel_id=1, source_target_pairs={{0,4},{1,13},{2,6},{3,15},{4,8},{5,1},{6,10},{7,3},{8,12},{9,5},{1... | collective-permute-start | bytes 1376264 | tf_op jit(solution)/shard_map/ppermute | solution.py:43
  2.4 20.9 %collective-permute-start.3 = (bf16[32,7168]{1,0:T(8,128)(2,1)}, bf16[32,7168]{1,0:T(8,128)(2,1)S(1)}, u32[]{:S(2)}, u32[]{:S(2)}) collective-permute-start(bf16[32,7168]{1,0:T(8,128)(2,1)} %bitcast.54), channel_id=1, source_target_pairs={{0,12},{1,5},{2,14},{3,7},{4,0},{5,9},{6,2},{7,11},{8,4},{9,13},{1... | collective-permute-start | bytes 1376264 | tf_op jit(solution)/shard_map/ppermute | solution.py:43
  7.0 0.7 copy-start.3
  7.7 0.7 copy-start.5
  8.3 7.0 %collective-permute-start = (bf16[256,256]{1,0:T(8,128)(2,1)S(1)}, bf16[256,256]{1,0:T(8,128)(2,1)S(1)}, u32[]{:S(2)}, u32[]{:S(2)}) collective-permute-start(bf16[256,256]{1,0:T(8,128)(2,1)S(1)} %get-tuple-element.40), channel_id=1, source_target_pairs={{0,1},{1,0},{2,3},{3,2},{4,5},{5,4},{6,7},{7,6},{8,9},{9,8},{10,11... | collective-permute-start | bytes 393224 | tf_op jit(solution)/shard_map/ppermute | solution.py:43
  8.3 35.9 %collective-permute-start.2 = (bf16[32,7168]{1,0:T(8,128)(2,1)}, bf16[32,7168]{1,0:T(8,128)(2,1)S(1)}, u32[]{:S(2)}, u32[]{:S(2)}) collective-permute-start(bf16[32,7168]{1,0:T(8,128)(2,1)} %bitcast.55), channel_id=1, source_target_pairs={{0,2},{1,3},{2,0},{3,1},{4,6},{5,7},{6,4},{7,5},{8,10},{9,11},{10,... | collective-permute-start | bytes 1376264 | tf_op jit(solution)/shard_map/ppermute | solution.py:43
  15.4 0.7 copy-start.7
  16.0 0.9 copy-start.6
  16.9 0.9 copy-start.8
  17.8 25.7 %copy-start.1 = (bf16[1,32,7168]{2,1,0:T(8,128)(2,1)S(1)}, bf16[1,32,7168]{2,1,0:T(8,128)(2,1)}, u32[]{:S(2)}) copy-start(bf16[1,32,7168]{2,1,0:T(8,128)(2,1)} %param.13) | copy-start | bytes 1376260
  22.8 19.9 %copy-start.2 = (bf16[32,7168]{1,0:T(8,128)(2,1)}, bf16[32,7168]{1,0:T(8,128)(2,1)S(1)}, u32[]{:S(2)}) copy-start(bf16[32,7168]{1,0:T(8,128)(2,1)S(1)} %get-tuple-element.42) | copy-start | bytes 1376260
  22.8 20.4 %copy-start.9 = (bf16[32,7168]{1,0:T(8,128)(2,1)}, bf16[32,7168]{1,0:T(8,128)(2,1)S(1)}, u32[]{:S(2)}) copy-start(bf16[32,7168]{1,0:T(8,128)(2,1)S(1)} %get-tuple-element.58) | copy-start | bytes 1376260
  22.8 20.4 %copy-start.11 = (bf16[32,7168]{1,0:T(8,128)(2,1)}, bf16[32,7168]{1,0:T(8,128)(2,1)S(1)}, u32[]{:S(2)}) copy-start(bf16[32,7168]{1,0:T(8,128)(2,1)S(1)} %get-tuple-element.49) | copy-start | bytes 1376260
  22.8 9.8 %collective-permute-start.10 = (bf16[32,7168]{1,0:T(8,128)(2,1)S(1)}, bf16[32,7168]{1,0:T(8,128)(2,1)S(1)}, u32[]{:S(2)}, u32[]{:S(2)}) collective-permute-start(bf16[32,7168]{1,0:T(8,128)(2,1)S(1)} %collective-permute-done.9.rest_1_), channel_id=1, source_target_pairs={{0,4},{1,13},{2,6},{3,15},{4,8},{5,1},{6,10},{7,3},{8,12},{9,5},{1... | collective-permute-start | bytes 1376264 | tf_op jit(solution)/shard_map/ppermute | solution.py:43
  23.3 16.5 %collective-permute-start.4 = (bf16[32,7168]{1,0:T(8,128)(2,1)S(1)}, bf16[32,7168]{1,0:T(8,128)(2,1)S(1)}, u32[]{:S(2)}, u32[]{:S(2)}) collective-permute-start(bf16[32,7168]{1,0:T(8,128)(2,1)S(1)} %get-tuple-element.46), channel_id=1, source_target_pairs={{0,4},{1,13},{2,6},{3,15},{4,8},{5,1},{6,10},{7,3},{8,12},{9,5},{1... | collective-permute-start | bytes 1376264 | tf_op jit(solution)/shard_map/ppermute | solution.py:43
  32.6 10.1 %collective-permute-start.11 = (bf16[32,7168]{1,0:T(8,128)(2,1)S(1)}, bf16[32,7168]{1,0:T(8,128)(2,1)S(1)}, u32[]{:S(2)}, u32[]{:S(2)}) collective-permute-start(bf16[32,7168]{1,0:T(8,128)(2,1)S(1)} %get-tuple-element.55), channel_id=1, source_target_pairs={{0,12},{1,5},{2,14},{3,7},{4,0},{5,9},{6,2},{7,11},{8,4},{9,13},{1... | collective-permute-start | bytes 1376264 | tf_op jit(solution)/shard_map/ppermute | solution.py:43
  34.3 6.4 %collective-permute-start.24 = (bf16[8,7168]{1,0:T(8,128)(2,1)S(1)}, bf16[8,7168]{1,0:T(8,128)(2,1)S(1)}, u32[]{:S(2)}, u32[]{:S(2)}) collective-permute-start(bf16[8,7168]{1,0:T(8,128)(2,1)S(1)} %dynamic-slice_bitcast_fusion), channel_id=1, source_target_pairs={{0,16},{16,0},{32,48},{48,32},{64,80},{80,64},{96,112},{112,96},{1... | collective-permute-start | bytes 344072 | tf_op jit(solution)/shard_map/ppermute | solution.py:43
  40.7 10.5 %collective-permute-start.5 = (bf16[32,7168]{1,0:T(8,128)(2,1)}, bf16[32,7168]{1,0:T(8,128)(2,1)}, u32[]{:S(2)}, u32[]{:S(2)}) collective-permute-start(bf16[32,7168]{1,0:T(8,128)(2,1)} %add_convert_fusion.3), channel_id=1, source_target_pairs={{0,4},{1,13},{2,6},{3,15},{4,8},{5,1},{6,10},{7,3},{8,12},{9,5},{1... | collective-permute-start | bytes 1376264 | tf_op jit(solution)/shard_map/ppermute | solution.py:43
  42.7 0.8 copy-start.12
  42.7 8.4 %collective-permute-start.25 = (bf16[8,7168]{1,0:T(8,128)(2,1)}, bf16[8,7168]{1,0:T(8,128)(2,1)}, u32[]{:S(2)}, u32[]{:S(2)}) collective-permute-start(bf16[8,7168]{1,0:T(8,128)(2,1)} %reduce-precision_convert_fusion.2), channel_id=1, source_target_pairs={{0,32},{16,48},{32,0},{48,16},{64,96},{80,112},{96,64},{112,80},{1... | collective-permute-start | bytes 344072 | tf_op jit(solution)/shard_map/ppermute | solution.py:43
  43.5 17.0 %collective-permute-start.16 = (bf16[32,7168]{1,0:T(8,128)(2,1)S(1)}, bf16[32,7168]{1,0:T(8,128)(2,1)}, u32[]{:S(2)}, u32[]{:S(2)}) collective-permute-start(bf16[32,7168]{1,0:T(8,128)(2,1)S(1)} %bitcast.56), channel_id=1, source_target_pairs={{0,1},{1,0},{2,3},{3,2},{4,5},{5,4},{6,7},{7,6},{8,9},{9,8},{10,11... | collective-permute-start | bytes 1376264 | tf_op jit(solution)/shard_map/ppermute | solution.py:43
  43.6 33.2 %copy-start.10 = (bf16[32,7168]{1,0:T(8,128)(2,1)S(1)}, bf16[32,7168]{1,0:T(8,128)(2,1)}, u32[]{:S(2)}) copy-start(bf16[32,7168]{1,0:T(8,128)(2,1)} %copy-done.9) | copy-start | bytes 1376260
  43.6 36.0 %copy-start.13 = (f32[2,8,7168]{2,1,0:T(8,128)S(1)}, f32[2,8,7168]{2,1,0:T(8,128)}, u32[]{:S(2)}) copy-start(f32[2,8,7168]{2,1,0:T(8,128)} %param.15) | copy-start | bytes 1376260
  43.6 36.0 %copy-start.14 = (f32[2,8,7168]{2,1,0:T(8,128)S(1)}, f32[2,8,7168]{2,1,0:T(8,128)}, u32[]{:S(2)}) copy-start(f32[2,8,7168]{2,1,0:T(8,128)} %param.16) | copy-start | bytes 1376260
  43.6 37.4 %copy-start.4 = (bf16[512,256]{1,0:T(8,128)(2,1)S(1)}, bf16[512,256]{1,0:T(8,128)(2,1)}, u32[]{:S(2)}) copy-start(bf16[512,256]{1,0:T(8,128)(2,1)} %copy-done.3) | copy-start | bytes 786436
  43.7 17.5 %collective-permute-start.17 = (bf16[32,7168]{1,0:T(8,128)(2,1)S(1)}, bf16[32,7168]{1,0:T(8,128)(2,1)S(1)}, u32[]{:S(2)}, u32[]{:S(2)}) collective-permute-start(bf16[32,7168]{1,0:T(8,128)(2,1)S(1)} %collective-permute-done.9.rest_1_), channel_id=1, source_target_pairs={{0,1},{1,0},{2,3},{3,2},{4,5},{5,4},{6,7},{7,6},{8,9},{9,8},{10,11... | collective-permute-start | bytes 1376264 | tf_op jit(solution)/shard_map/ppermute | solution.py:43
  44.3 16.1 %collective-permute-start.12 = (bf16[32,7168]{1,0:T(8,128)(2,1)S(1)}, bf16[32,7168]{1,0:T(8,128)(2,1)S(1)}, u32[]{:S(2)}, u32[]{:S(2)}) collective-permute-start(bf16[32,7168]{1,0:T(8,128)(2,1)S(1)} %collective-permute-done.2.rest_4_), channel_id=1, source_target_pairs={{0,4},{1,13},{2,6},{3,15},{4,8},{5,1},{6,10},{7,3},{8,12},{9,5},{1... | collective-permute-start | bytes 1376264 | tf_op jit(solution)/shard_map/ppermute | solution.py:43
  51.1 9.3 %collective-permute-start.6 = (bf16[32,7168]{1,0:T(8,128)(2,1)S(1)}, bf16[32,7168]{1,0:T(8,128)(2,1)S(1)}, u32[]{:S(2)}, u32[]{:S(2)}) collective-permute-start(bf16[32,7168]{1,0:T(8,128)(2,1)S(1)} %collective-permute-done.2.rest_4_), channel_id=1, source_target_pairs={{0,12},{1,5},{2,14},{3,7},{4,0},{5,9},{6,2},{7,11},{8,4},{9,13},{1... | collective-permute-start | bytes 1376264 | tf_op jit(solution)/shard_map/ppermute | solution.py:43
  52.1 8.3 %collective-permute-start.26 = (bf16[8,7168]{1,0:T(8,128)(2,1)S(1)}, bf16[8,7168]{1,0:T(8,128)(2,1)S(1)}, u32[]{:S(2)}, u32[]{:S(2)}) collective-permute-start(bf16[8,7168]{1,0:T(8,128)(2,1)S(1)} %reduce-precision_convert_fusion.1), channel_id=1, source_target_pairs={{0,64},{16,80},{32,96},{48,112},{64,0},{80,16},{96,32},{112,48},{1... | collective-permute-start | bytes 344072 | tf_op jit(solution)/shard_map/ppermute | solution.py:43
  60.4 15.7 %collective-permute-start.18 = (bf16[32,7168]{1,0:T(8,128)(2,1)S(1)}, bf16[32,7168]{1,0:T(8,128)(2,1)S(1)}, u32[]{:S(2)}, u32[]{:S(2)}) collective-permute-start(bf16[32,7168]{1,0:T(8,128)(2,1)S(1)} %collective-permute-done.3.rest_2_), channel_id=1, source_target_pairs={{0,1},{1,0},{2,3},{3,2},{4,5},{5,4},{6,7},{7,6},{8,9},{9,8},{10,11... | collective-permute-start | bytes 1376264 | tf_op jit(solution)/shard_map/ppermute | solution.py:43
  60.4 9.7 %collective-permute-start.13 = (bf16[32,7168]{1,0:T(8,128)(2,1)S(1)}, bf16[32,7168]{1,0:T(8,128)(2,1)S(1)}, u32[]{:S(2)}, u32[]{:S(2)}) collective-permute-start(bf16[32,7168]{1,0:T(8,128)(2,1)S(1)} %collective-permute-done.12.rest_5_), channel_id=1, source_target_pairs={{0,4},{1,13},{2,6},{3,15},{4,8},{5,1},{6,10},{7,3},{8,12},{9,5},{1... | collective-permute-start | bytes 1376264 | tf_op jit(solution)/shard_map/ppermute | solution.py:43
  60.4 14.6 %collective-permute-start.7 = (bf16[32,7168]{1,0:T(8,128)(2,1)}, bf16[32,7168]{1,0:T(8,128)(2,1)S(1)}, u32[]{:S(2)}, u32[]{:S(2)}) collective-permute-start(bf16[32,7168]{1,0:T(8,128)(2,1)} %copy-done.11), channel_id=1, source_target_pairs={{0,4},{1,13},{2,6},{3,15},{4,8},{5,1},{6,10},{7,3},{8,12},{9,5},{1... | collective-permute-start | bytes 1376264 | tf_op jit(solution)/shard_map/ppermute | solution.py:43
  60.6 15.7 %collective-permute-start.20 = (bf16[32,7168]{1,0:T(8,128)(2,1)S(1)}, bf16[32,7168]{1,0:T(8,128)(2,1)S(1)}, u32[]{:S(2)}, u32[]{:S(2)}) collective-permute-start(bf16[32,7168]{1,0:T(8,128)(2,1)S(1)} %collective-permute-done.2.rest_4_), channel_id=1, source_target_pairs={{0,1},{1,0},{2,3},{3,2},{4,5},{5,4},{6,7},{7,6},{8,9},{9,8},{10,11... | collective-permute-start | bytes 1376264 | tf_op jit(solution)/shard_map/ppermute | solution.py:43
  61.1 15.7 %collective-permute-start.19 = (bf16[32,7168]{1,0:T(8,128)(2,1)S(1)}, bf16[32,7168]{1,0:T(8,128)(2,1)S(1)}, u32[]{:S(2)}, u32[]{:S(2)}) collective-permute-start(bf16[32,7168]{1,0:T(8,128)(2,1)S(1)} %collective-permute-done.10.rest_3_), channel_id=1, source_target_pairs={{0,1},{1,0},{2,3},{3,2},{4,5},{5,4},{6,7},{7,6},{8,9},{9,8},{10,11... | collective-permute-start | bytes 1376264 | tf_op jit(solution)/shard_map/ppermute | solution.py:43
  70.1 6.8 %collective-permute-start.27 = (bf16[8,7168]{1,0:T(8,128)(2,1)S(1)}, bf16[8,7168]{1,0:T(8,128)(2,1)S(1)}, u32[]{:S(2)}, u32[]{:S(2)}) collective-permute-start(bf16[8,7168]{1,0:T(8,128)(2,1)S(1)} %reduce-precision_convert_fusion), channel_id=1, source_target_pairs={{0,128},{16,144},{32,160},{48,176},{64,192},{80,208},{96,224},{112... | collective-permute-start | bytes 344072 | tf_op jit(solution)/shard_map/ppermute | solution.py:43
  75.0 3.9 %collective-permute-start.21 = (bf16[32,7168]{1,0:T(8,128)(2,1)S(1)}, bf16[32,7168]{1,0:T(8,128)(2,1)S(1)}, u32[]{:S(2)}, u32[]{:S(2)}) collective-permute-start(bf16[32,7168]{1,0:T(8,128)(2,1)S(1)} %collective-permute-done.12.rest_5_), channel_id=1, source_target_pairs={{0,1},{1,0},{2,3},{3,2},{4,5},{5,4},{6,7},{7,6},{8,9},{9,8},{10,11... | collective-permute-start | bytes 1376264 | tf_op jit(solution)/shard_map/ppermute | solution.py:43
  76.1 26.8 %collective-permute-start.15 = (bf16[32,7168]{1,0:T(8,128)(2,1)S(1)}, bf16[32,7168]{1,0:T(8,128)(2,1)S(1)}, u32[]{:S(2)}, u32[]{:S(2)}) collective-permute-start(bf16[32,7168]{1,0:T(8,128)(2,1)S(1)} %add_convert_fusion.1), channel_id=1, source_target_pairs={{0,2},{1,3},{2,0},{3,1},{4,6},{5,7},{6,4},{7,5},{8,10},{9,11},{10,... | collective-permute-start | bytes 1376264 | tf_op jit(solution)/shard_map/ppermute | solution.py:43
  76.3 4.2 %collective-permute-start.22 = (bf16[32,7168]{1,0:T(8,128)(2,1)S(1)}, bf16[32,7168]{1,0:T(8,128)(2,1)S(1)}, u32[]{:S(2)}, u32[]{:S(2)}) collective-permute-start(bf16[32,7168]{1,0:T(8,128)(2,1)S(1)} %collective-permute-done.6.rest_6_), channel_id=1, source_target_pairs={{0,1},{1,0},{2,3},{3,2},{4,5},{5,4},{6,7},{7,6},{8,9},{9,8},{10,11... | collective-permute-start | bytes 1376264 | tf_op jit(solution)/shard_map/ppermute | solution.py:43
  76.9 26.0 %collective-permute-start.14 = (bf16[32,7168]{1,0:T(8,128)(2,1)S(1)}, bf16[32,7168]{1,0:T(8,128)(2,1)S(1)}, u32[]{:S(2)}, u32[]{:S(2)}) collective-permute-start(bf16[32,7168]{1,0:T(8,128)(2,1)S(1)} %copy-done.10), channel_id=1, source_target_pairs={{0,12},{1,5},{2,14},{3,7},{4,0},{5,9},{6,2},{7,11},{8,4},{9,13},{1... | collective-permute-start | bytes 1376264 | tf_op jit(solution)/shard_map/ppermute | solution.py:43
  76.9 26.0 %collective-permute-start.8 = (bf16[32,7168]{1,0:T(8,128)(2,1)S(1)}, bf16[32,7168]{1,0:T(8,128)(2,1)S(1)}, u32[]{:S(2)}, u32[]{:S(2)}) collective-permute-start(bf16[32,7168]{1,0:T(8,128)(2,1)S(1)} %add_convert_fusion.2), channel_id=1, source_target_pairs={{0,4},{1,13},{2,6},{3,15},{4,8},{5,1},{6,10},{7,3},{8,12},{9,5},{1... | collective-permute-start | bytes 1376264 | tf_op jit(solution)/shard_map/ppermute | solution.py:43
  78.9 2.2 %collective-permute-start.23 = (bf16[32,7168]{1,0:T(8,128)(2,1)S(1)}, bf16[32,7168]{1,0:T(8,128)(2,1)S(1)}, u32[]{:S(2)}, u32[]{:S(2)}) collective-permute-start(bf16[32,7168]{1,0:T(8,128)(2,1)S(1)} %collective-permute-done.13.rest_7_), channel_id=1, source_target_pairs={{0,1},{1,0},{2,3},{3,2},{4,5},{5,4},{6,7},{7,6},{8,9},{9,8},{10,11... | collective-permute-start | bytes 1376264 | tf_op jit(solution)/shard_map/ppermute | solution.py:43
